TPU v7x, 256 devices: a whole 4x4x8 slice. The times are simulated.
256 devices in a mesh: az: 64 (over x, y_hi, z), ax: 4 (over y_lo, core).
Axes of the slice: x: 4, y: 4 (y_hi: 2, y_lo: 2; y = y_hi * 2 + y_lo), z: 8, core: 2. Of those that a mesh axis runs over, the one named last changes fastest.
Arguments:
- fields: float32 [5, 64, 1024, 512], P(None, 'ax', 'az'), may hold values from -6.5 to 6.5, as said below
Outputs:
- advanced: float32 [5, 64, 1024, 512], P(None, 'ax', 'az')
Inputs may be any that keep to these rules, and one draw needn't show every extreme that they name: `fields`: each field is a rough part plus, on every axial plane and cycle, a constant and a first azimuthal harmonic.
All inputs are finite; a program needn't handle non-finite values.
Results may differ from a plain program's by a relative error of at most 0.0003.
Values sent between devices are 32-bit elements; how exact they have to be, the bound alone decides.
A program may use at most 128 MiB of HBM per device.

v0:
```python
import jax
import jax.numpy as jnp
from jax import lax
from jax.sharding import PartitionSpec as P

NEAR = 40


viscosity = 0.2
time_step = 0.1
buoyancy = 1.0


def swapped(block, axis, distance):
    count = lax.axis_size(axis)
    route = []
    for low in range(count):
        high = low | 1 << distance
        if high != low and high < count:
            route += [(low, high), (high, low)]
    return lax.ppermute(block, axis, route)


def with_halo(block, sides, width, periodic):
    for axis, dim in sides:
        count = lax.axis_size(axis)
        forward = [(i, i + 1) for i in range(count - 1)]
        if periodic:
            forward.append((count - 1, 0))
        backward = [(target, source) for source, target in forward]
        low = lax.ppermute(
            lax.slice_in_dim(block, block.shape[dim] - width, None, axis=dim), axis, forward
        )
        high = lax.ppermute(lax.slice_in_dim(block, 0, width, axis=dim), axis, backward)
        block = jnp.concatenate([low, block, high], axis=dim)
    return block


def mode_tables(theta_index, total_theta, modes):
    column = jnp.arange(modes, dtype=jnp.int32)
    product = theta_index[:, None] * column[None, :] % total_theta
    angle = product.astype(jnp.float32) * (2.0 * jnp.pi / total_theta)
    cosine = jnp.cos(angle)
    sine = jnp.sin(angle)
    weight = jnp.where(column == 0, 1.0, 2.0).astype(jnp.float32) / total_theta
    forward = jnp.concatenate([cosine * weight[None, :], sine * (2.0 / total_theta)], axis=1)
    inverse = jnp.concatenate([cosine, sine], axis=1)
    return (forward, inverse)


def cycle_mask(cycles, modes):
    cycle_index = jnp.arange(cycles, dtype=jnp.int32)
    cutoff = jnp.minimum(355 * (2 * cycle_index + 1) // 226, modes - 1)
    column = jnp.arange(modes, dtype=jnp.int32)
    keep = (column[None, :] <= cutoff[:, None]).astype(jnp.float32)
    return jnp.concatenate([keep, keep], axis=1)


def operators(
    center, radial_plus, radial_minus, theta_plus, theta_minus, axial_plus, axial_minus, total_theta
):
    radius = jnp.arange(center.shape[-1], dtype=jnp.float32) + 0.5
    step_angle = 2.0 * jnp.pi / total_theta
    d_radial = (radial_plus - radial_minus) * 0.5
    d_theta = (theta_plus - theta_minus) / (2.0 * step_angle)
    d_axial = (axial_plus - axial_minus) * 0.5
    laplace = (
        radial_plus - 2.0 * center + radial_minus + (radial_plus - radial_minus) / (2.0 * radius)
    )
    laplace = laplace + (theta_plus - 2.0 * center + theta_minus) / (
        radius * radius * step_angle * step_angle
    )
    laplace = laplace + axial_plus - 2.0 * center + axial_minus
    return (d_radial, d_theta, d_axial, laplace)


def on_device(fields):
    count_fields, planes, theta_dev, radial = fields.shape
    sectors = lax.axis_size("az")
    total_theta = theta_dev * sectors
    modes = min(128, total_theta // 2)
    sector = lax.axis_index("az")
    own_index = sector * theta_dev + jnp.arange(theta_dev, dtype=jnp.int32)
    own_forward, own_inverse = mode_tables(own_index, total_theta, modes)
    inner_cycles = fields[:, :, :, :NEAR]
    kept = None
    piece = lax.all_gather(inner_cycles, "az", axis=2, tiled=True)
    piece_index = jnp.arange(piece.shape[2], dtype=jnp.int32)
    piece_forward, unused_inverse = mode_tables(piece_index, total_theta, modes)
    spectra = jnp.einsum("fztj,tc->fzjc", piece, piece_forward, precision=lax.Precision.HIGHEST)
    kept = spectra * cycle_mask(NEAR, modes)[None, None]
    smoothed = jnp.einsum("fzjc,tc->fztj", kept, own_inverse, precision=lax.Precision.HIGHEST)
    state = jnp.concatenate([smoothed, fields[:, :, :, NEAR:]], axis=3)
    flip = jnp.array([-1.0, -1.0, 1.0, 1.0, 1.0], dtype=jnp.float32)[:, None, None]
    top_bit = sectors.bit_length() - 1
    opposite = swapped(state[:, :, :, 0], "az", top_bit - 1)
    opposite = opposite * flip
    theta_padded = with_halo(state, (("az", 2),), 1, True)
    axial_padded = with_halo(state, (("ax", 1),), 1, False)
    radial_plus = jnp.concatenate([state[:, :, :, 1:], jnp.zeros_like(state[:, :, :, :1])], axis=3)
    radial_minus = jnp.concatenate([opposite[:, :, :, None], state[:, :, :, :-1]], axis=3)
    d_radial, d_theta, d_axial, laplace = operators(
        state,
        radial_plus,
        radial_minus,
        theta_padded[:, :, 2:, :],
        theta_padded[:, :, :-2, :],
        axial_padded[:, 2:, :, :],
        axial_padded[:, :-2, :, :],
        total_theta,
    )
    radius = jnp.arange(radial, dtype=jnp.float32) + 0.5
    radial_u = state[0]
    theta_u = state[1]
    axial_u = state[2]
    change = (
        -(radial_u[None] * d_radial + (theta_u / radius)[None] * d_theta + axial_u[None] * d_axial)
        + viscosity * laplace
    )
    inverse_square = 1.0 / (radius * radius)
    first = (
        change[0]
        + theta_u * theta_u / radius
        - viscosity * (radial_u * inverse_square + 2.0 * inverse_square * d_theta[1])
    )
    second = (
        change[1]
        - radial_u * theta_u / radius
        - viscosity * (theta_u * inverse_square - 2.0 * inverse_square * d_theta[0])
    )
    third = change[2] + buoyancy * state[3]
    change = jnp.concatenate([first[None], second[None], third[None], change[3:]], axis=0)
    return state + time_step * change


def solution(mesh):
    placed = (P(None, "ax", "az", None),)
    return jax.shard_map(
        on_device, mesh=mesh, in_specs=placed, out_specs=P(None, "ax", "az", None), check_vma=False
    )
```

profile of v0, /device:TPU:1, one launch (start us, length us, event | category | flops | bytes accessed | tf_op | source)
XLA Modules:
  0.0 499.4 jit_solution(17314941103463150801)
XLA Ops:
  6.5 2.0 slice.73
  8.6 4.0 slice.74
  12.5 3.2 copy.19
  16.1 3.0 sine_multiply_fusion
  19.1 355.6 %all-gather.2.cloned.1.call-done = f32[5,16,1024,40]{3,2,1,0:T(8,128)} async-done(((f32[5,16,16,40]{3,2,1,0:T(8,128)}), f32[5,16,1024,40]{3,2,1,0:T(8,128)}) %all-gather.2.cloned.1.call-update) | async-done | bytes 13107216 | tf_op jit(solution)/shard_map/all_gather | solution.py:87
  374.7 70.2 %fusion.8 = f32[256,5,16,40]{0,3,2,1:T(8,128)S(1)} fusion(f32[5,16,1024,40]{3,2,1,0:T(8,128)} %all-gather.2.cloned.1.call-done, f32[1024,128]{1,0:T(8,128)S(1)} %get-tuple-element.19, f32[1024,128]{1,0:T(8,128)} %get-tuple-element.20), kind=kOutput, calls=%fused_computation.40 | convolution fusion | flops 10066591744 | bytes 17432576 | tf_op jit(solution)/shard_map/fztj,tc->fzjc/dot_general | solution.py:90
  444.9 5.4 %fusion.7 = f32[5,16,16,40]{3,2,1,0:T(8,128)S(1)} fusion(f32[256,5,16,40]{0,3,2,1:T(8,128)S(1)} %fusion.8, f32[40,256]{1,0:T(8,128)S(1)} %add_convert_fusion, f32[16,128]{1,0:T(8,128)S(1)} %get-tuple-element.18, f32[16,128]{1,0:T(8,128)S(1)} %get-tuple-element.17), kind=kOutput, calls=%fused_computation.38 | convolution fusion | flops 158109696 | bytes 3538944 | tf_op jit(solution)/shard_map/fzjc,tc->fztj/dot_general | solution.py:92
  450.5 0.9 fusion.33
  451.4 3.9 fusion.1
  455.6 1.6 multiply_bitcast_fusion.1
  457.2 2.7 collective-permute-start
  459.9 0.7 fusion.31
  460.6 2.3 collective-permute-start.1
  463.6 6.0 %collective-permute-start.3 = (f32[5,1,16,512]{3,2,1,0:T(8,128)}, f32[5,1,16,512]{3,2,1,0:T(8,128)}, u32[]{:S(2)}, u32[]{:S(2)}) collective-permute-start(f32[5,1,16,512]{3,2,1,0:T(8,128)} %copy.12), channel_id=1, source_target_pairs={{1,0},{2,1},{3,2},{5,4},{6,5},{7,6},{9,8},{10,9},{11,10},{13,12},{... | collective-permute-start | bytes 491528 | tf_op jit(solution)/shard_map/ppermute | solution.py:34
  470.2 3.0 collective-permute-start.4
  473.3 1.4 copy.11
  474.7 1.3 collective-permute-done.3
  476.0 1.1 copy.13
  477.1 1.1 copy.15
  478.2 7.4 %multiply_add_fusion = f32[5,16,16,512]{3,1,2,0:T(8,128)S(1)} fusion(f32[5,1,16,512]{3,1,2,0:T(1,128)S(1)} %copy.13, f32[5,16,16,472]{3,1,2,0:T(8,128)S(1)} %copy.19, f32[5,16,16,40]{3,1,2,0:T(8,128)S(1)} %copy.10, f32[5,1,16,512]{3,1,2,0:T(1,128)S(1)} %copy.15, f32[5,16,16,511]{3,1,2,0:T(8,128)} %get-tuple-element.14, f32[5,16,16,1]{3,1,2,0:T(8,128)} %copy.11, ...), kind=kLoop, calls=%fused_computation.26 | loop fusion | flops 21626880 | bytes 12712960 | tf_op jit(solution)/shard_map/add | solution.py:117
  485.7 2.3 fusion.6
  488.0 0.8 fusion.26
  488.8 0.8 fusion.3
  489.6 3.0 copy.16
  (24 shorter events, 2.3 us)
Async XLA Ops:
  6.5 368.2 %all-gather.2.cloned.1.call-start = ((), (), s32[]{:S(2)}) async-start(), calls=%async_computation | async-start | bytes 42598400 | tf_op jit(solution)/shard_map/all_gather | solution.py:87
  457.2 16.1 %copy-start = (f32[5]{0:T(128)S(1)}, f32[5]{0:T(128)}, u32[]{:S(2)}) copy-start(f32[5]{0:T(128)} %constant.82.clone) | copy-start | bytes 64
  457.2 16.1 %collective-permute-start = (f32[5,16,16]{2,1,0:T(8,128)S(1)}, f32[5,16,16]{2,1,0:T(8,128)S(1)}, u32[]{:S(2)}, u32[]{:S(2)}) collective-permute-start(f32[5,16,16]{2,1,0:T(8,128)S(1)} %slice_reduce_fusion), channel_id=1, source_target_pairs={{0,128},{128,0},{4,132},{132,4},{8,136},{136,8},{12,140},{140,12},... | collective-permute-start | bytes 15368 | tf_op jit(solution)/shard_map/ppermute | solution.py:21
  460.6 17.6 %collective-permute-start.1 = (f32[5,16,1,512]{3,1,2,0:T(8,128)}, f32[5,16,1,512]{3,1,2,0:T(8,128)S(1)}, u32[]{:S(2)}, u32[]{:S(2)}) collective-permute-start(f32[5,16,1,512]{3,1,2,0:T(8,128)} %get-tuple-element.12), channel_id=1, source_target_pairs={{4,0},{8,4},{12,8},{16,12},{20,16},{24,20},{28,24},{32,28},{36,32}... | collective-permute-start | bytes 491528 | tf_op jit(solution)/shard_map/ppermute | solution.py:34
  462.9 15.3 %collective-permute-start.2 = (f32[5,16,1,512]{3,1,2,0:T(8,128)}, f32[5,16,1,512]{3,1,2,0:T(8,128)}, u32[]{:S(2)}, u32[]{:S(2)}) collective-permute-start(f32[5,16,1,512]{3,1,2,0:T(8,128)} %get-tuple-element.11), channel_id=1, source_target_pairs={{0,4},{4,8},{8,12},{12,16},{16,20},{20,24},{24,28},{28,32},{32,36}... | collective-permute-start | bytes 491528 | tf_op jit(solution)/shard_map/ppermute | solution.py:31
  463.6 12.4 %collective-permute-start.3 = (f32[5,1,16,512]{3,2,1,0:T(8,128)}, f32[5,1,16,512]{3,2,1,0:T(8,128)}, u32[]{:S(2)}, u32[]{:S(2)}) collective-permute-start(f32[5,1,16,512]{3,2,1,0:T(8,128)} %copy.12), channel_id=1, source_target_pairs={{1,0},{2,1},{3,2},{5,4},{6,5},{7,6},{9,8},{10,9},{11,10},{13,12},{... | collective-permute-start | bytes 491528 | tf_op jit(solution)/shard_map/ppermute | solution.py:34
  470.2 6.9 %collective-permute-start.4 = (f32[5,1,16,512]{3,2,1,0:T(8,128)}, f32[5,1,16,512]{3,2,1,0:T(8,128)}, u32[]{:S(2)}, u32[]{:S(2)}) collective-permute-start(f32[5,1,16,512]{3,2,1,0:T(8,128)} %copy.14), channel_id=1, source_target_pairs={{0,1},{1,2},{2,3},{4,5},{5,6},{6,7},{8,9},{9,10},{10,11},{12,13},{... | collective-permute-start | bytes 491528 | tf_op jit(solution)/shard_map/ppermute | solution.py:31
Sparse Core Ops, SparseCore 0:
  10.8 363.8 all-gather.1
where the time goes:
time: 500 us; the launch traced here: 499 us
  waiting for transfers between devices  357 us (71%)
  matrix products  75.6 us (15%)
  other arithmetic  21.8 us (4%)
  local copies, waits for them, and re-layouts  17.6 us (4%)
  starting transfers between devices  13.9 us (3%)
  between operations  13.6 us (3%)
    all_gather x1, waiting for transfers between devices, on_device(): piece = lax.all_gather(inner_cycles, 'az', axis=2, tiled=True)  356 us
    dot_general x1, matrix products, on_device(): jnp.einsum('fztj,tc->fzjc', piece, piece_forward, precision=lax.Precision...  70.2 us
  transfers between devices with their start and end apart: 6, of which 2 were waited for; matrix products, arithmetic and copies ran while one was open for 3% of the time, Pallas kernels for 0%

commit v1 on v0

--- a/solution.py
+++ b/solution.py
@@ -1,14 +1,214 @@
+import functools
+
 import jax
 import jax.numpy as jnp
+import ml_dtypes
+import numpy as np
 from jax import lax
+from jax.experimental import pallas as pl
+from jax.experimental.pallas import tpu as pltpu
 from jax.sharding import PartitionSpec as P
 
 NEAR = 40
-
+FIELDS = 5
+MODES = 128
+LANES = 128
+HALF = 64
+QUARTER = 10
+MESH = pl.DeviceIdType.MESH
 
 viscosity = 0.2
 time_step = 0.1
 buoyancy = 1.0
+
+
+def split(table, pieces):
+    out = []
+    rest = table.astype(np.float32)
+    for _ in range(pieces):
+        piece = rest.astype(ml_dtypes.bfloat16)
+        out.append(piece)
+        rest = rest - piece.astype(np.float32)
+    return np.stack(out)
+
+
+def transform_tables(sectors, theta_dev):
+    total = sectors * theta_dev
+    half = theta_dev // 2
+    theta = (
+        np.arange(sectors)[None, :, None] * theta_dev
+        + np.arange(2)[:, None, None] * half
+        + np.arange(half)[None, None, :]
+    ).reshape(2, sectors * half)
+    mode = np.arange(MODES)
+    angle = (theta[:, :, None] * mode[None, None, :] % total) * (2.0 * np.pi / total)
+    basis = np.concatenate([np.cos(angle), np.sin(angle)], axis=2)
+    weight = np.concatenate([np.where(mode == 0, 1.0, 2.0), np.full(MODES, 2.0)]) / total
+    forward = (basis * weight).transpose(0, 2, 1).reshape(4 * MODES, sectors * half)
+    inverse = basis.transpose(1, 0, 2).reshape(sectors * half, 4 * MODES)
+    return split(forward, 2), split(inverse, 3)
+
+
+def filter_kernel(
+    sectors,
+    fields,
+    forward_hbm,
+    inverse_hbm,
+    near,
+    raw,
+    forward,
+    inverse,
+    send1,
+    recv1,
+    send2,
+    recv2,
+    load_sem,
+    send_sem1,
+    recv_sem1,
+    send_sem2,
+    recv_sem2,
+):
+    me = lax.axis_index("az")
+    planes = raw.shape[1]
+    half = raw.shape[2] // 2
+    load = pltpu.make_async_copy(fields.at[:, :, :, pl.ds(0, LANES)], raw, load_sem.at[0])
+    load.start()
+    load_forward = pltpu.make_async_copy(forward_hbm, forward, load_sem.at[1])
+    load_forward.start()
+    load_inverse = pltpu.make_async_copy(inverse_hbm, inverse, load_sem.at[2])
+    load_inverse.start()
+    barrier = pltpu.get_barrier_semaphore()
+
+    def greet(i, carry):
+        pl.semaphore_signal(
+            barrier, inc=1, device_id={"az": (me + i) % sectors}, device_id_type=MESH
+        )
+        return carry
+
+    lax.fori_loop(1, sectors, greet, 0)
+    load.wait()
+    lane = lax.broadcasted_iota(jnp.int32, (half, LANES), 1)
+
+    def pack(k, carry):
+        tail0 = raw[4, k, :half, :]
+        tail1 = raw[4, k, half:, :]
+        for f in range(4):
+            shift = NEAR - QUARTER * f
+            first = jnp.where(lane < NEAR, raw[f, k, :half, :], pltpu.roll(tail0, shift, 1))
+            second = jnp.where(lane < NEAR, raw[f, k, half:, :], pltpu.roll(tail1, shift, 1))
+            send1[k * 4 + f] = jnp.where(lane < HALF, first, pltpu.roll(second, HALF, 1))
+        return carry
+
+    lax.fori_loop(0, planes, pack, 0)
+    pl.semaphore_wait(barrier, sectors - 1)
+
+    def exchange(source, target, send_sem, recv_sem):
+        def post(i, carry):
+            peer = (me + i) % sectors
+            pltpu.make_async_remote_copy(
+                src_ref=source.at[peer],
+                dst_ref=target.at[me],
+                send_sem=send_sem,
+                recv_sem=recv_sem,
+                device_id={"az": peer},
+                device_id_type=MESH,
+            ).start()
+            return carry
+
+        lax.fori_loop(1, sectors, post, 0)
+        target[me] = source[me]
+        return pltpu.make_async_remote_copy(
+            src_ref=source.at[pl.ds(0, sectors - 1)],
+            dst_ref=target.at[pl.ds(0, sectors - 1)],
+            send_sem=send_sem,
+            recv_sem=recv_sem,
+            device_id={"az": (me + 1) % sectors},
+            device_id_type=MESH,
+        )
+
+    first = exchange(send1, recv1, send_sem1, recv_sem1)
+    load_forward.wait()
+    load_inverse.wait()
+    first.wait_recv()
+    values = recv1[...].reshape(sectors * half, LANES)
+    high = values.astype(jnp.bfloat16)
+    low = (values - high.astype(jnp.float32)).astype(jnp.bfloat16)
+    dot = functools.partial(jnp.dot, preferred_element_type=jnp.float32)
+    spectra = dot(forward[0], high) + (dot(forward[0], low) + dot(forward[1], high))
+    row = lax.broadcasted_iota(jnp.int32, (2 * MODES, LANES), 0)
+    column = lax.broadcasted_iota(jnp.int32, (2 * MODES, LANES), 1)
+    spectra = jnp.where(column < HALF, spectra[: 2 * MODES], spectra[2 * MODES :])
+    spectra = spectra + pltpu.roll(spectra, HALF, 1)
+    slot = jnp.where(column < HALF, column, column - HALF)
+    cycle = jnp.where(slot < NEAR, slot, slot - NEAR + QUARTER * (me % 4))
+    cutoff = jnp.floor((355 * (2 * cycle + 1)).astype(jnp.float32) / 226.0 + 0.001)
+    mode = jnp.where(row < MODES, row, row - MODES).astype(jnp.float32)
+    spectra = jnp.where(mode <= jnp.minimum(cutoff, MODES - 1.0), spectra, 0.0)
+    spectra = jnp.concatenate(
+        [jnp.where(column < HALF, spectra, 0.0), jnp.where(column < HALF, 0.0, spectra)], axis=0
+    )
+    high = spectra.astype(jnp.bfloat16)
+    rest = spectra - high.astype(jnp.float32)
+    middle = rest.astype(jnp.bfloat16)
+    low = (rest - middle.astype(jnp.float32)).astype(jnp.bfloat16)
+    smooth = dot(inverse[0], low) + dot(inverse[1], middle) + dot(inverse[2], high)
+    smooth = smooth + (dot(inverse[0], middle) + dot(inverse[1], high))
+    smooth = smooth + dot(inverse[0], high)
+    send2[...] = smooth.reshape(sectors, half, LANES)
+    second = exchange(send2, recv2, send_sem2, recv_sem2)
+    second.wait_recv()
+
+    def unpack(k, carry):
+        tail0 = raw[4, k, :half, :]
+        tail1 = raw[4, k, half:, :]
+        for f in range(4):
+            got = recv2[k * 4 + f]
+            near[f, k, :half, :] = jnp.where(lane < NEAR, got, raw[f, k, :half, :])
+            near[f, k, half:, :] = jnp.where(
+                lane < NEAR, pltpu.roll(got, HALF, 1), raw[f, k, half:, :]
+            )
+            here = (lane >= QUARTER * f) & (lane < QUARTER * (f + 1))
+            shift = (QUARTER * f - NEAR) % LANES
+            tail0 = jnp.where(here, pltpu.roll(got, shift, 1), tail0)
+            tail1 = jnp.where(here, pltpu.roll(got, (shift + HALF) % LANES, 1), tail1)
+        near[4, k, :half, :] = tail0
+        near[4, k, half:, :] = tail1
+        return carry
+
+    lax.fori_loop(0, planes, unpack, 0)
+    first.wait_send()
+    second.wait_send()
+
+
+def filtered(fields, sectors):
+    count, planes, theta_dev, radial = fields.shape
+    half = theta_dev // 2
+    forward, inverse = transform_tables(sectors, theta_dev)
+    any_spec = pl.BlockSpec(memory_space=pl.ANY)
+    return pl.pallas_call(
+        functools.partial(filter_kernel, sectors),
+        out_shape=jax.ShapeDtypeStruct((count, planes, theta_dev, LANES), jnp.float32),
+        in_specs=[any_spec, any_spec, any_spec],
+        out_specs=pl.BlockSpec(memory_space=pltpu.VMEM),
+        scratch_shapes=[
+            pltpu.VMEM((count, planes, theta_dev, LANES), jnp.float32),
+            pltpu.VMEM(forward.shape, jnp.bfloat16),
+            pltpu.VMEM(inverse.shape, jnp.bfloat16),
+            pltpu.VMEM((sectors, half, LANES), jnp.float32),
+            pltpu.VMEM((sectors, half, LANES), jnp.float32),
+            pltpu.VMEM((sectors, half, LANES), jnp.float32),
+            pltpu.VMEM((sectors, half, LANES), jnp.float32),
+            pltpu.SemaphoreType.DMA((3,)),
+            pltpu.SemaphoreType.DMA,
+            pltpu.SemaphoreType.DMA,
+            pltpu.SemaphoreType.DMA,
+            pltpu.SemaphoreType.DMA,
+        ],
+        compiler_params=pltpu.CompilerParams(
+            collective_id=0, has_side_effects=True, vmem_limit_bytes=48 << 20
+        ),
+        name="azimuthal_filter",
+    )(fields, jnp.asarray(forward), jnp.asarray(inverse))
 
 
 def swapped(block, axis, distance):
@@ -36,26 +236,6 @@
     return block
 
 
-def mode_tables(theta_index, total_theta, modes):
-    column = jnp.arange(modes, dtype=jnp.int32)
-    product = theta_index[:, None] * column[None, :] % total_theta
-    angle = product.astype(jnp.float32) * (2.0 * jnp.pi / total_theta)
-    cosine = jnp.cos(angle)
-    sine = jnp.sin(angle)
-    weight = jnp.where(column == 0, 1.0, 2.0).astype(jnp.float32) / total_theta
-    forward = jnp.concatenate([cosine * weight[None, :], sine * (2.0 / total_theta)], axis=1)
-    inverse = jnp.concatenate([cosine, sine], axis=1)
-    return (forward, inverse)
-
-
-def cycle_mask(cycles, modes):
-    cycle_index = jnp.arange(cycles, dtype=jnp.int32)
-    cutoff = jnp.minimum(355 * (2 * cycle_index + 1) // 226, modes - 1)
-    column = jnp.arange(modes, dtype=jnp.int32)
-    keep = (column[None, :] <= cutoff[:, None]).astype(jnp.float32)
-    return jnp.concatenate([keep, keep], axis=1)
-
-
 def operators(
     center, radial_plus, radial_minus, theta_plus, theta_minus, axial_plus, axial_minus, total_theta
 ):
@@ -78,19 +258,8 @@
     count_fields, planes, theta_dev, radial = fields.shape
     sectors = lax.axis_size("az")
     total_theta = theta_dev * sectors
-    modes = min(128, total_theta // 2)
-    sector = lax.axis_index("az")
-    own_index = sector * theta_dev + jnp.arange(theta_dev, dtype=jnp.int32)
-    own_forward, own_inverse = mode_tables(own_index, total_theta, modes)
-    inner_cycles = fields[:, :, :, :NEAR]
-    kept = None
-    piece = lax.all_gather(inner_cycles, "az", axis=2, tiled=True)
-    piece_index = jnp.arange(piece.shape[2], dtype=jnp.int32)
-    piece_forward, unused_inverse = mode_tables(piece_index, total_theta, modes)
-    spectra = jnp.einsum("fztj,tc->fzjc", piece, piece_forward, precision=lax.Precision.HIGHEST)
-    kept = spectra * cycle_mask(NEAR, modes)[None, None]
-    smoothed = jnp.einsum("fzjc,tc->fztj", kept, own_inverse, precision=lax.Precision.HIGHEST)
-    state = jnp.concatenate([smoothed, fields[:, :, :, NEAR:]], axis=3)
+    near = filtered(fields, sectors)
+    state = jnp.concatenate([near, fields[:, :, :, LANES:]], axis=3)
     flip = jnp.array([-1.0, -1.0, 1.0, 1.0, 1.0], dtype=jnp.float32)[:, None, None]
     top_bit = sectors.bit_length() - 1
     opposite = swapped(state[:, :, :, 0], "az", top_bit - 1)

time: 500 us -> 71.6 us (0.14)
  waiting for transfers between devices: 357 us -> 0.01 us
  matrix products: 75.6 us -> 0 us
  Pallas kernels: 0 us -> 33.6 us
  between operations: 13.6 us -> 0.15 us
  other arithmetic: 21.8 us -> 9.43 us
    all_gather x1 -> x0, waiting for transfers between devices: 356 us -> none  [on_device(): piece = lax.all_gather(inner_cycles, 'az', axis=2, tiled=True)]
    dot_general x2 -> x0, matrix products: 75.6 us -> none  [the longest x1 70.2 us: on_device(): jnp.einsum('fztj,tc->fzjc', piece, piece_forward, precision=lax.Precision...]
    pallas_call x0 -> x1, Pallas kernels: none -> 33.6 us  [filtered(): pl.pallas_call(functools.partial(filter_kernel, sectors), out_shape=jax.S...]
    concatenate x4 -> x0, other arithmetic: 5.55 us -> none  [the longest x3 5.55 us: on_device(): state = jnp.concatenate([smoothed, fields[:, :, :, NEAR:]], axis=3)]
  transfers between devices with their start and end apart: 6 -> 5, of which waited for: 2 -> 0; matrix products, arithmetic and copies ran while one was open for 3% -> 13% of each run, Pallas kernels for 0% -> 0%
where the time goes in v1:
time: 71.6 us; the launch traced here: 71.4 us
  Pallas kernels  33.6 us (47%)
  local copies, waits for them, and re-layouts  16 us (22%)
  starting transfers between devices  12.1 us (17%)
  other arithmetic  9.43 us (13%)
    pallas_call x1, Pallas kernels, filtered(): pl.pallas_call(functools.partial(filter_kernel, sectors), out_shape=jax.S...  33.6 us
    ppermute x2, starting transfers between devices, with_halo(): lax.ppermute(lax.slice_in_dim(block, 0, width, axis=dim), axis, backward)  7.72 us
    add x1, other arithmetic, on_device(): -(radial_u[None] * d_radial + (theta_u / radius)[None] * d_theta + axial_...  5.4 us
    unnamed x9, local copies, waits for them, and re-layouts  3.68 us
    slice x1, local copies, waits for them, and re-layouts, on_device(): state[:, :, :, 1:]  3.28 us
    ppermute x2, starting transfers between devices, with_halo(): lax.ppermute(lax.slice_in_dim(block, block.shape[dim] - width, None, axis...  3.28 us
    add x1, local copies, waits for them, and re-layouts, on_device(): return state + time_step * change  2.98 us
    slice x3, local copies, waits for them, and re-layouts, with_halo(): lax.slice_in_dim(block, block.shape[dim] - width, None, axis=dim)  1.73 us
  transfers between devices with their start and end apart: 5, of which 0 were waited for; matrix products, arithmetic and copies ran while one was open for 13% of the time, Pallas kernels for 0%

profile of v1, /device:TPU:1, one launch (start us, length us, event | category | flops | bytes accessed | tf_op | source)
XLA Modules:
  0.0 71.4 jit_solution(7544378726023126501)
XLA Ops:
  0.0 1.2 %copy-done.2 = bf16[2,512,512]{2,1,0:T(8,128)(2,1)S(1)} copy-done((bf16[2,512,512]{2,1,0:T(8,128)(2,1)S(1)}, bf16[2,512,512]{2,1,0:T(8,128)(2,1)}, u32[]{:S(2)}) %copy-start.2) | copy-done | bytes 1048600
  1.2 0.8 %copy-done = f32[5,16,16,512]{3,2,1,0:T(8,128)S(1)} copy-done((f32[5,16,16,512]{3,2,1,0:T(8,128)S(1)}, f32[5,16,16,512]{3,2,1,0:T(8,128)}, u32[]{:S(2)}) %copy-start) | copy-done | bytes 2621464
  2.1 1.4 %copy-done.1 = bf16[3,512,512]{2,1,0:T(8,128)(2,1)S(1)} copy-done((bf16[3,512,512]{2,1,0:T(8,128)(2,1)S(1)}, bf16[3,512,512]{2,1,0:T(8,128)(2,1)}, u32[]{:S(2)}) %copy-start.1) | copy-done | bytes 1572888
  3.5 33.6 %azimuthal_filter.1 = f32[5,16,16,128]{3,2,1,0:T(8,128)S(1)} custom-call(f32[5,16,16,512]{3,2,1,0:T(8,128)S(1)} %copy-done, bf16[2,512,512]{2,1,0:T(8,128)(2,1)S(1)} %copy-done.2, bf16[3,512,512]{2,1,0:T(8,128)(2,1)S(1)} %copy-done.1), custom_call_target="tpu_custom_call" | custom-call | tf_op jit(solution)/shard_map/azimuthal_filter/pallas_call | solution.py:188
  37.3 0.6 copy_dynamic-update-slice_fusion
  37.9 0.8 %fusion.11 = (f32[5,16,1,512]{3,1,2,0:T(8,128)}, f32[5,16,1,512]{3,1,2,0:T(8,128)}) fusion(f32[5,16,16,512]{3,1,2,0:T(8,128)S(1)} %copy_dynamic-update-slice_fusion), kind=kLoop, calls=%fused_computation.34 | loop fusion | bytes 655360 | tf_op jit(solution)/shard_map/slice | solution.py:232
  38.7 3.3 %collective-permute-start.1 = (f32[5,16,1,512]{3,1,2,0:T(8,128)}, f32[5,16,1,512]{3,1,2,0:T(8,128)S(1)}, u32[]{:S(2)}, u32[]{:S(2)}) collective-permute-start(f32[5,16,1,512]{3,1,2,0:T(8,128)} %get-tuple-element.12), channel_id=1, source_target_pairs={{4,0},{8,4},{12,8},{16,12},{20,16},{24,20},{28,24},{32,28},{36,32}... | collective-permute-start | bytes 491528 | tf_op jit(solution)/shard_map/ppermute | solution.py:234
  42.0 0.3 fusion.13
  42.4 0.7 copy.14
  43.0 4.4 %collective-permute-start.3 = (f32[5,1,16,512]{3,2,1,0:T(8,128)}, f32[5,1,16,512]{3,2,1,0:T(8,128)}, u32[]{:S(2)}, u32[]{:S(2)}) collective-permute-start(f32[5,1,16,512]{3,2,1,0:T(8,128)} %copy.14), channel_id=1, source_target_pairs={{1,0},{2,1},{3,2},{5,4},{6,5},{7,6},{9,8},{10,9},{11,10},{13,12},{... | collective-permute-start | bytes 491528 | tf_op jit(solution)/shard_map/ppermute | solution.py:234
  47.4 0.7 copy.16
  48.1 3.3 %collective-permute-start.4 = (f32[5,1,16,512]{3,2,1,0:T(8,128)}, f32[5,1,16,512]{3,2,1,0:T(8,128)}, u32[]{:S(2)}, u32[]{:S(2)}) collective-permute-start(f32[5,1,16,512]{3,2,1,0:T(8,128)} %copy.16), channel_id=1, source_target_pairs={{0,1},{1,2},{2,3},{4,5},{5,6},{6,7},{8,9},{9,10},{10,11},{12,13},{... | collective-permute-start | bytes 491528 | tf_op jit(solution)/shard_map/ppermute | solution.py:231
  51.4 0.2 slice_reduce_fusion
  51.6 1.1 %collective-permute-start = (f32[5,16,16]{2,1,0:T(8,128)S(1)}, f32[5,16,16]{2,1,0:T(8,128)S(1)}, u32[]{:S(2)}, u32[]{:S(2)}) collective-permute-start(f32[5,16,16]{2,1,0:T(8,128)S(1)} %slice_reduce_fusion), channel_id=1, source_target_pairs={{0,128},{128,0},{4,132},{132,4},{8,136},{136,8},{12,140},{140,12},... | collective-permute-start | bytes 15368 | tf_op jit(solution)/shard_map/ppermute | solution.py:221
  52.8 3.3 %fusion.12 = (f32[5,16,16,511]{3,1,2,0:T(8,128)}, f32[5,16,16,511]{3,1,2,0:T(8,128)}) fusion(f32[5,16,16,512]{3,1,2,0:T(8,128)S(1)} %copy_dynamic-update-slice_fusion), kind=kLoop, calls=%fused_computation.35 | loop fusion | bytes 10465280 | tf_op jit(solution)/shard_map/slice | solution.py:269
  56.1 1.2 %multiply_bitcast_fusion.1 = (f32[16,16,512]{2,0,1:T(8,128)}, f32[16,16,512]{2,0,1:T(8,128)}, f32[16,16,512]{2,0,1:T(8,128)}) fusion(f32[5,16,16,512]{3,1,2,0:T(8,128)S(1)} %copy_dynamic-update-slice_fusion, f32[512]{0:T(512)S(1)} %get-tuple-element.19), kind=kLoop, calls=%fused_computation.27 | loop fusion | flops 524288 | bytes 3147776 | tf_op jit(solution)/shard_map/mul | solution.py:286
  57.4 0.6 copy.13
  57.9 1.1 %copy.15 = f32[5,1,16,512]{3,1,2,0:T(1,128)S(1)} copy(f32[5,1,16,512]{3,2,1,0:T(8,128)} %collective-permute-done.3) | data formatting | bytes 327680 | tf_op jit(solution)/shard_map/ppermute | solution.py:234
  59.0 1.1 %copy.17 = f32[5,1,16,512]{3,1,2,0:T(1,128)S(1)} copy(f32[5,1,16,512]{3,2,1,0:T(8,128)} %collective-permute-done.4) | data formatting | bytes 327680 | tf_op jit(solution)/shard_map/ppermute | solution.py:231
  60.1 5.4 %multiply_add_fusion = f32[5,16,16,512]{3,1,2,0:T(8,128)S(1)} fusion(f32[5,16,16,512]{3,1,2,0:T(8,128)S(1)} %copy_dynamic-update-slice_fusion, f32[5,1,16,512]{3,1,2,0:T(1,128)S(1)} %copy.15, f32[5,1,16,512]{3,1,2,0:T(1,128)S(1)} %copy.17, f32[5,16,16,511]{3,1,2,0:T(8,128)} %get-tuple-element.14, f32[5,16,16,1]{3,1,2,0:T(8,128)S(1)} %copy.13, ...), kind=kLoop, calls=%fused_computation.7 | loop fusion | flops 18350080 | bytes 12712960 | tf_op jit(solution)/shard_map/add | solution.py:286
  65.7 1.5 %fusion.2 = f32[5,16,16,512]{3,1,2,0:T(8,128)S(1)} fusion(f32[5,16,1,512]{3,1,2,0:T(8,128)S(1)} %collective-permute-done.1, f32[5,16,16,512]{3,1,2,0:T(8,128)S(1)} %copy_dynamic-update-slice_fusion, f32[5,16,1,512]{3,1,2,0:T(8,128)} %collective-permute-done.2), kind=kLoop, calls=%fused_computation.9 | loop fusion | flops 2621440 | bytes 5570560 | tf_op jit(solution)/shard_map/div | solution.py:245
  67.2 0.5 fusion.8
  67.8 0.6 fusion
  68.4 3.0 %copy.18 = f32[5,16,16,512]{3,2,1,0:T(8,128)} copy(f32[5,16,16,512]{3,1,2,0:T(8,128)S(1)} %fusion) | data formatting | bytes 5242880 | tf_op jit(solution)/shard_map/add | solution.py:302
  (19 shorter events, 0.4 us)
Async XLA Ops:
  0.0 1.2 %copy-start.2 = (bf16[2,512,512]{2,1,0:T(8,128)(2,1)S(1)}, bf16[2,512,512]{2,1,0:T(8,128)(2,1)}, u32[]{:S(2)}) copy-start(bf16[2,512,512]{2,1,0:T(8,128)(2,1)} %constant.10.clone.forward_hbm) | copy-start | bytes 3145732
  0.0 2.1 %copy-start = (f32[5,16,16,512]{3,2,1,0:T(8,128)S(1)}, f32[5,16,16,512]{3,2,1,0:T(8,128)}, u32[]{:S(2)}) copy-start(f32[5,16,16,512]{3,2,1,0:T(8,128)} %fields.1) | copy-start | bytes 7864324
  2.1 1.4 %copy-start.1 = (bf16[3,512,512]{2,1,0:T(8,128)(2,1)S(1)}, bf16[3,512,512]{2,1,0:T(8,128)(2,1)}, u32[]{:S(2)}) copy-start(bf16[3,512,512]{2,1,0:T(8,128)(2,1)} %constant.28.clone.inverse_hbm) | copy-start | bytes 4718596
  3.5 33.8 %slice-start = ((f32[5,16,16,512]{3,2,1,0:T(8,128)}), f32[5,16,16,384]{3,2,1,0:T(8,128)S(1)}, s32[]{:S(2)}) async-start(f32[5,16,16,512]{3,2,1,0:T(8,128)} %fields.1), calls=%async_computation | async-start | bytes 3932160 | tf_op jit(solution)/shard_map/slice | solution.py:262
  38.7 21.4 %collective-permute-start.1 = (f32[5,16,1,512]{3,1,2,0:T(8,128)}, f32[5,16,1,512]{3,1,2,0:T(8,128)S(1)}, u32[]{:S(2)}, u32[]{:S(2)}) collective-permute-start(f32[5,16,1,512]{3,1,2,0:T(8,128)} %get-tuple-element.12), channel_id=1, source_target_pairs={{4,0},{8,4},{12,8},{16,12},{20,16},{24,20},{28,24},{32,28},{36,32}... | collective-permute-start | bytes 491528 | tf_op jit(solution)/shard_map/ppermute | solution.py:234
  42.0 18.1 %collective-permute-start.2 = (f32[5,16,1,512]{3,1,2,0:T(8,128)}, f32[5,16,1,512]{3,1,2,0:T(8,128)}, u32[]{:S(2)}, u32[]{:S(2)}) collective-permute-start(f32[5,16,1,512]{3,1,2,0:T(8,128)} %get-tuple-element.11), channel_id=1, source_target_pairs={{0,4},{4,8},{8,12},{12,16},{16,20},{20,24},{24,28},{28,32},{32,36}... | collective-permute-start | bytes 491528 | tf_op jit(solution)/shard_map/ppermute | solution.py:231
  43.0 14.9 %collective-permute-start.3 = (f32[5,1,16,512]{3,2,1,0:T(8,128)}, f32[5,1,16,512]{3,2,1,0:T(8,128)}, u32[]{:S(2)}, u32[]{:S(2)}) collective-permute-start(f32[5,1,16,512]{3,2,1,0:T(8,128)} %copy.14), channel_id=1, source_target_pairs={{1,0},{2,1},{3,2},{5,4},{6,5},{7,6},{9,8},{10,9},{11,10},{13,12},{... | collective-permute-start | bytes 491528 | tf_op jit(solution)/shard_map/ppermute | solution.py:234
  48.1 11.0 %collective-permute-start.4 = (f32[5,1,16,512]{3,2,1,0:T(8,128)}, f32[5,1,16,512]{3,2,1,0:T(8,128)}, u32[]{:S(2)}, u32[]{:S(2)}) collective-permute-start(f32[5,1,16,512]{3,2,1,0:T(8,128)} %copy.16), channel_id=1, source_target_pairs={{0,1},{1,2},{2,3},{4,5},{5,6},{6,7},{8,9},{9,10},{10,11},{12,13},{... | collective-permute-start | bytes 491528 | tf_op jit(solution)/shard_map/ppermute | solution.py:231
  51.6 5.7 %collective-permute-start = (f32[5,16,16]{2,1,0:T(8,128)S(1)}, f32[5,16,16]{2,1,0:T(8,128)S(1)}, u32[]{:S(2)}, u32[]{:S(2)}) collective-permute-start(f32[5,16,16]{2,1,0:T(8,128)S(1)} %slice_reduce_fusion), channel_id=1, source_target_pairs={{0,128},{128,0},{4,132},{132,4},{8,136},{136,8},{12,140},{140,12},... | collective-permute-start | bytes 15368 | tf_op jit(solution)/shard_map/ppermute | solution.py:221
  56.0 1.3 %copy-start.3 = (f32[5]{0:T(128)S(1)}, f32[5]{0:T(128)}, u32[]{:S(2)}) copy-start(f32[5]{0:T(128)} %constant.29.clone) | copy-start | bytes 64

commit v2 on v1

v2 whole, which is shorter than its diff:
```python
import functools

import jax
import jax.numpy as jnp
import ml_dtypes
import numpy as np
from jax import lax
from jax.experimental import pallas as pl
from jax.experimental.pallas import tpu as pltpu
from jax.sharding import PartitionSpec as P

NEAR = 40
FIELDS = 5
MODES = 128
LANES = 128
HALF = 64
QUARTER = 10
TOP = 8
MESH = pl.DeviceIdType.MESH

viscosity = 0.2
time_step = 0.1
buoyancy = 1.0


def split(table, pieces):
    out = []
    rest = table.astype(np.float32)
    for _ in range(pieces):
        piece = rest.astype(ml_dtypes.bfloat16)
        out.append(piece)
        rest = rest - piece.astype(np.float32)
    return np.stack(out)


def basis(theta, total):
    mode = np.arange(MODES)
    angle = (theta[..., None] * mode % total) * (2.0 * np.pi / total)
    return np.concatenate([np.cos(angle), np.sin(angle)], axis=-1)


def transform_tables(sectors, theta_dev):
    total = sectors * theta_dev
    half = theta_dev // 2
    sector = np.arange(sectors)[:, None] * theta_dev
    mode = np.arange(MODES)
    weight = np.concatenate([np.where(mode == 0, 1.0, 2.0), np.full(MODES, 2.0)]) / total
    forward = []
    inverse = []
    for side in range(2):
        theta = (sector + side * half + np.arange(half)).reshape(-1)
        forward.append((basis(theta, total) * weight).T)
        first = sector + (half if side else -1)
        theta = np.concatenate([(first + np.arange(half)).reshape(-1), (first + half).reshape(-1)])
        inverse.append(basis(theta, total))
    return split(np.concatenate(forward, axis=0), 2), split(np.concatenate(inverse, axis=1), 3)


def stencil_kernel(
    sectors,
    slabs,
    fields,
    forward_hbm,
    inverse_hbm,
    advanced,
    state,
    across,
    result,
    forward,
    inverse,
    send1,
    recv1,
    send2,
    recv2,
    extra,
    edge_send,
    edge_recv,
    load_sem,
    store_sem,
    send_sem,
    recv_sem,
):
    me = lax.axis_index("az")
    slab = lax.axis_index("ax")
    planes = fields.shape[1]
    theta_dev = fields.shape[2]
    half = theta_dev // 2
    tiles = fields.shape[3] // LANES
    body = pl.ds(TOP, theta_dev)
    middle = TOP + half
    step_angle = 2.0 * np.pi / (sectors * theta_dev)

    loads = []
    for tile in range(tiles):
        loads.append(
            pltpu.make_async_copy(
                fields.at[:, :, :, pl.ds(tile * LANES, LANES)],
                state.at[tile, :, pl.ds(1, planes), body, :],
                load_sem.at[tile],
            )
        )
        loads[-1].start()
    load_forward = pltpu.make_async_copy(forward_hbm, forward, load_sem.at[tiles])
    load_forward.start()
    load_inverse = pltpu.make_async_copy(inverse_hbm, inverse, load_sem.at[tiles + 1])
    load_inverse.start()

    barrier = pltpu.get_barrier_semaphore()

    def greet(i, carry):
        pl.semaphore_signal(
            barrier, inc=1, device_id={"az": (me + i) % sectors}, device_id_type=MESH
        )
        return carry

    lax.fori_loop(1, sectors, greet, 0)
    above = (slab + 1) % slabs
    below = (slab + slabs - 1) % slabs
    for neighbour in (above, below):
        pl.semaphore_signal(barrier, inc=1, device_id={"ax": neighbour}, device_id_type=MESH)

    loads[0].wait()
    lane = lax.broadcasted_iota(jnp.int32, (half, LANES), 1)
    lane_row = lax.broadcasted_iota(jnp.int32, (1, LANES), 1)

    def pack(k, carry):
        tail0 = state[0, 4, k + 1, TOP:middle, :]
        tail1 = state[0, 4, k + 1, middle : middle + half, :]
        for f in range(4):
            shift = NEAR - QUARTER * f
            first = jnp.where(
                lane < NEAR, state[0, f, k + 1, TOP:middle, :], pltpu.roll(tail0, shift, 1)
            )
            second = jnp.where(
                lane < NEAR,
                state[0, f, k + 1, middle : middle + half, :],
                pltpu.roll(tail1, shift, 1),
            )
            send1[k * 4 + f] = jnp.where(lane < HALF, first, pltpu.roll(second, HALF, 1))
        return carry

    lax.fori_loop(0, planes, pack, 0)
    pl.semaphore_wait(barrier, sectors + 1)

    def exchange(source, target, index):
        def post(i, carry):
            peer = (me + i) % sectors
            pltpu.make_async_remote_copy(
                src_ref=source.at[peer],
                dst_ref=target.at[me],
                send_sem=send_sem.at[index],
                recv_sem=recv_sem.at[index],
                device_id={"az": peer},
                device_id_type=MESH,
            ).start()
            return carry

        lax.fori_loop(1, sectors, post, 0)
        target[me] = source[me]
        return pltpu.make_async_remote_copy(
            src_ref=source.at[pl.ds(0, sectors - 1)],
            dst_ref=target.at[pl.ds(0, sectors - 1)],
            send_sem=send_sem.at[index],
            recv_sem=recv_sem.at[index],
            device_id={"az": (me + 1) % sectors},
            device_id_type=MESH,
        )

    first_exchange = exchange(send1, recv1, 0)

    def plane_copy(first_tile, count, source, target, neighbour, index):
        return pltpu.make_async_remote_copy(
            src_ref=state.at[pl.ds(first_tile, count), :, source, body, :],
            dst_ref=state.at[pl.ds(first_tile, count), :, target, body, :],
            send_sem=send_sem.at[index],
            recv_sem=recv_sem.at[index],
            device_id={"ax": neighbour},
            device_id_type=MESH,
        )

    for load in loads[1:]:
        load.wait()
    far_planes = [
        plane_copy(1, tiles - 1, planes, 0, above, 2),
        plane_copy(1, tiles - 1, 1, planes + 1, below, 3),
    ]
    for copy in far_planes:
        copy.start()

    def collect(i, carry):
        tile = i // FIELDS
        f = i % FIELDS
        for k in range(planes):
            edge_send[0, tile, f, k : k + 1, :] = state[tile, f, k + 1, TOP : TOP + 1, :]
            edge_send[1, tile, f, k : k + 1, :] = state[
                tile, f, k + 1, TOP + theta_dev - 1 : TOP + theta_dev, :
            ]
        return carry

    lax.fori_loop(0, tiles * FIELDS, collect, 0)
    edges = []
    for side, peer in ((0, (me + sectors - 1) % sectors), (1, (me + 1) % sectors)):
        edges.append(
            pltpu.make_async_remote_copy(
                src_ref=edge_send.at[side],
                dst_ref=edge_recv.at[side],
                send_sem=send_sem.at[4 + side],
                recv_sem=recv_sem.at[4 + side],
                device_id={"az": peer},
                device_id_type=MESH,
            )
        )
        edges[-1].start()

    load_forward.wait()
    load_inverse.wait()
    first_exchange.wait_recv()
    values = recv1[...].reshape(sectors * half, LANES)
    high = values.astype(jnp.bfloat16)
    low = (values - high.astype(jnp.float32)).astype(jnp.bfloat16)
    dot = functools.partial(jnp.dot, preferred_element_type=jnp.float32)
    spectra = dot(forward[0], high) + (dot(forward[0], low) + dot(forward[1], high))
    row = lax.broadcasted_iota(jnp.int32, (2 * MODES, LANES), 0)
    column = lax.broadcasted_iota(jnp.int32, (2 * MODES, LANES), 1)
    spectra = jnp.where(column < HALF, spectra[: 2 * MODES], spectra[2 * MODES :])
    spectra = spectra + pltpu.roll(spectra, HALF, 1)
    slot = jnp.where(column < HALF, column, column - HALF)
    group = me % 4
    cycle = jnp.where(slot < NEAR, slot, slot - NEAR + QUARTER * group)
    cutoff = jnp.floor((355 * (2 * cycle + 1)).astype(jnp.float32) / 226.0 + 0.001)
    mode = jnp.where(row < MODES, row, row - MODES)
    kept = mode.astype(jnp.float32) <= jnp.minimum(cutoff, MODES - 1.0)
    spectra = jnp.where(kept, spectra, 0.0)
    parity = jnp.where(mode % 2 == 0, 1.0, -1.0)
    vector_sign = jnp.where(group < 2, -1.0, 1.0)
    spectra = jnp.where(
        slot == HALF - 1,
        parity * vector_sign * pltpu.roll(spectra, HALF - 1, 1),
        jnp.where(slot == HALF - 2, parity * pltpu.roll(spectra, HALF - 2 - NEAR, 1), spectra),
    )
    spectra = jnp.concatenate(
        [jnp.where(column < HALF, spectra, 0.0), jnp.where(column < HALF, 0.0, spectra)], axis=0
    )
    high = spectra.astype(jnp.bfloat16)
    rest = spectra - high.astype(jnp.float32)
    medium = rest.astype(jnp.bfloat16)
    low = (rest - medium.astype(jnp.float32)).astype(jnp.bfloat16)
    smooth = dot(inverse[0], low) + dot(inverse[1], medium) + dot(inverse[2], high)
    smooth = smooth + (dot(inverse[0], medium) + dot(inverse[1], high))
    smooth = smooth + dot(inverse[0], high)
    send2[:, 0:half, :] = smooth[: sectors * half].reshape(sectors, half, LANES)
    extra[...] = smooth[sectors * half :]

    def last_rows(i, carry):
        for d in range(8):
            send2[i * 8 + d, half : half + 1, :] = extra[pl.ds(i * 8 + d, 1), :]
        return carry

    lax.fori_loop(0, sectors // 8, last_rows, 0)
    second_exchange = exchange(send2, recv2, 1)

    for copy in edges + far_planes:
        copy.wait_recv()

    def spread(i, carry):
        tile = i // FIELDS
        f = i % FIELDS
        for k in range(planes):
            state[tile, f, k + 1, TOP - 1 : TOP, :] = edge_recv[1, tile, f, k : k + 1, :]
            state[tile, f, k + 1, TOP + theta_dev : TOP + theta_dev + 1, :] = edge_recv[
                0, tile, f, k : k + 1, :
            ]
        return carry

    lax.fori_loop(0, tiles * FIELDS, spread, 0)

    def close(first_tile, last_tile):
        nothing = jnp.zeros((theta_dev, LANES), jnp.float32)
        for plane, edge in ((0, 0), (planes + 1, slabs - 1)):

            @pl.when(slab == edge)
            def _():
                for tile in range(first_tile, last_tile):
                    for f in range(FIELDS):
                        state[tile, f, plane, body, :] = nothing

    close(1, tiles)
    lane_full = lax.broadcasted_iota(jnp.int32, (theta_dev, LANES), 1)

    def advance(tile, k):
        radius = (lane_row + tile * LANES).astype(jnp.float32) + 0.5
        inverse_radius = 1.0 / radius
        inverse_square = 1.0 / (radius * radius)
        spread_rate = time_step * viscosity
        radial_base = (0.5 * spread_rate) * inverse_radius
        theta_rate = (-time_step / (2.0 * step_angle)) * inverse_radius
        theta_spread = (spread_rate / (step_angle * step_angle)) * inverse_square
        turn_rate = time_step * inverse_radius
        swirl = spread_rate * inverse_square
        cross = (spread_rate / step_angle) * inverse_square
        center = [state[tile, f, k + 1, body, :] for f in range(FIELDS)]
        radial = radial_base - (0.5 * time_step) * center[0]
        around = theta_rate * center[1]
        axial = (-0.5 * time_step) * center[2]
        outs = []
        turns = []
        for f in range(FIELDS):
            q = center[f]
            inner = across[f, k] if tile == 0 else state[tile - 1, f, k + 1, body, :]
            outer = 0.0 if tile == tiles - 1 else state[tile + 1, f, k + 1, body, :]
            minus = pltpu.roll(jnp.where(lane_full == LANES - 1, inner, q), 1, 1)
            plus = pltpu.roll(jnp.where(lane_full == 0, outer, q), LANES - 1, 1)
            ahead = state[tile, f, k + 1, pl.ds(TOP + 1, theta_dev), :] - q
            behind = state[tile, f, k + 1, pl.ds(TOP - 1, theta_dev), :] - q
            up = state[tile, f, k + 2, body, :]
            down = state[tile, f, k, body, :]
            turn = ahead - behind
            turns.append(turn)
            out = q + (plus - minus) * radial + turn * around + (up - down) * axial
            out = out + spread_rate * ((plus + minus) + (up + down) - 4.0 * q)
            outs.append(out + theta_spread * (ahead + behind))
        whirl = turn_rate * center[1]
        outs[0] = outs[0] + whirl * center[1] - swirl * center[0] - cross * turns[1]
        outs[1] = outs[1] - whirl * center[0] - swirl * center[1] + cross * turns[0]
        outs[2] = outs[2] + (time_step * buoyancy) * center[3]
        for f in range(FIELDS):
            result[tile, f, k] = outs[f]

    stores = []

    def store(tile):
        stores.append(
            pltpu.make_async_copy(
                result.at[tile],
                advanced.at[:, :, :, pl.ds(tile * LANES, LANES)],
                store_sem.at[tile],
            )
        )
        stores[-1].start()

    for tile in range(1, tiles):

        def far(k, carry):
            advance(tile, k)
            return carry

        lax.fori_loop(0, planes, far, 0)
        store(tile)

    second_exchange.wait_recv()

    def unpack(k):
        tail = [
            state[0, 4, k + 1, TOP:middle, :],
            state[0, 4, k + 1, middle : middle + half, :],
            state[0, 4, k + 1, TOP - 1 : TOP, :],
            state[0, 4, k + 1, TOP + theta_dev : TOP + theta_dev + 1, :],
        ]
        for f in range(4):
            got0 = recv2[k * 4 + f, 1 : half + 1, :]
            got1 = recv2[k * 4 + f, 0:half, :]
            got2 = recv2[k * 4 + f, 0:1, :]
            got3 = recv2[k * 4 + f, half : half + 1, :]
            turned = pltpu.roll(got1, HALF, 1)
            across[f, k, 0:half, :] = pltpu.roll(got0, HALF, 1)
            across[f, k, half:, :] = got1
            near = lane < NEAR
            near_row = lane_row < NEAR
            here = state.at[0, f, k + 1]
            here[TOP:middle, :] = jnp.where(near, got0, here[TOP:middle, :])
            here[middle : middle + half, :] = jnp.where(
                near, turned, here[middle : middle + half, :]
            )
            here[TOP - 1 : TOP, :] = jnp.where(near_row, got2, here[TOP - 1 : TOP, :])
            here[TOP + theta_dev : TOP + theta_dev + 1, :] = jnp.where(
                near_row,
                pltpu.roll(got3, HALF, 1),
                here[TOP + theta_dev : TOP + theta_dev + 1, :],
            )
            shift = (QUARTER * f - NEAR) % LANES
            other = (shift + HALF) % LANES
            part = (lane >= QUARTER * f) & (lane < QUARTER * (f + 1))
            part_row = (lane_row >= QUARTER * f) & (lane_row < QUARTER * (f + 1))
            tail[0] = jnp.where(part, pltpu.roll(got0, shift, 1), tail[0])
            tail[1] = jnp.where(part, pltpu.roll(got1, other, 1), tail[1])
            tail[2] = jnp.where(part_row, pltpu.roll(got2, shift, 1), tail[2])
            tail[3] = jnp.where(part_row, pltpu.roll(got3, other, 1), tail[3])
            if f == 0:
                across[4, k, 0:half, :] = pltpu.roll(got0, HALF + 1, 1)
                across[4, k, half:, :] = pltpu.roll(got1, 1, 1)
        state[0, 4, k + 1, TOP:middle, :] = tail[0]
        state[0, 4, k + 1, middle : middle + half, :] = tail[1]
        state[0, 4, k + 1, TOP - 1 : TOP, :] = tail[2]
        state[0, 4, k + 1, TOP + theta_dev : TOP + theta_dev + 1, :] = tail[3]

    unpack(0)
    unpack(planes - 1)
    near_planes = [
        plane_copy(0, 1, planes, 0, above, 6),
        plane_copy(0, 1, 1, planes + 1, below, 7),
    ]
    for copy in near_planes:
        copy.start()

    def unpack_inner(k, carry):
        unpack(k)
        return carry

    lax.fori_loop(1, planes - 1, unpack_inner, 0)

    def near(k, carry):
        advance(0, k)
        return carry

    lax.fori_loop(1, planes - 1, near, 0)
    for copy in near_planes:
        copy.wait_recv()
    close(0, 1)
    advance(0, 0)
    advance(0, planes - 1)
    store(0)
    first_exchange.wait_send()
    second_exchange.wait_send()
    for copy in edges + far_planes + near_planes:
        copy.wait_send()
    for copy in stores:
        copy.wait()


def on_device(fields):
    sectors = lax.axis_size("az")
    slabs = lax.axis_size("ax")
    count, planes, theta_dev, radial = fields.shape
    half = theta_dev // 2
    tiles = radial // LANES
    forward, inverse = transform_tables(sectors, theta_dev)
    hbm = pl.BlockSpec(memory_space=pltpu.HBM)
    return pl.pallas_call(
        functools.partial(stencil_kernel, sectors, slabs),
        out_shape=jax.ShapeDtypeStruct(fields.shape, jnp.float32),
        in_specs=[hbm, hbm, hbm],
        out_specs=hbm,
        scratch_shapes=[
            pltpu.VMEM((tiles, count, planes + 2, theta_dev + 2 * TOP, LANES), jnp.float32),
            pltpu.VMEM((count, planes, theta_dev, LANES), jnp.float32),
            pltpu.VMEM((tiles, count, planes, theta_dev, LANES), jnp.float32),
            pltpu.VMEM(forward.shape, jnp.bfloat16),
            pltpu.VMEM(inverse.shape, jnp.bfloat16),
            pltpu.VMEM((sectors, half, LANES), jnp.float32),
            pltpu.VMEM((sectors, half, LANES), jnp.float32),
            pltpu.VMEM((sectors, half + 1, LANES), jnp.float32),
            pltpu.VMEM((sectors, half + 1, LANES), jnp.float32),
            pltpu.VMEM((sectors, LANES), jnp.float32),
            pltpu.VMEM((2, tiles, count, planes, LANES), jnp.float32),
            pltpu.VMEM((2, tiles, count, planes, LANES), jnp.float32),
            pltpu.SemaphoreType.DMA((tiles + 2,)),
            pltpu.SemaphoreType.DMA((tiles,)),
            pltpu.SemaphoreType.DMA((8,)),
            pltpu.SemaphoreType.DMA((8,)),
        ],
        compiler_params=pltpu.CompilerParams(
            collective_id=0, has_side_effects=True, vmem_limit_bytes=48 << 20
        ),
        name="plume_section",
    )(fields, jnp.asarray(forward), jnp.asarray(inverse))


def solution(mesh):
    placed = (P(None, "ax", "az", None),)
    return jax.shard_map(
        on_device, mesh=mesh, in_specs=placed, out_specs=P(None, "ax", "az", None), check_vma=False
    )
```

time: 71.6 us -> 43.9 us (0.61)
  starting transfers between devices: 12.1 us -> 0 us
  local copies, waits for them, and re-layouts: 16 us -> 4.19 us
  other arithmetic: 9.43 us -> 0 us
  Pallas kernels: 33.6 us -> 39.6 us
    ppermute x5 -> x0, starting transfers between devices: 12.1 us -> none  [the longest x2 7.72 us: with_halo(): lax.ppermute(lax.slice_in_dim(block, 0, width, axis=dim), axis, backward)]
    slice x9 -> x0, local copies, waits for them, and re-layouts: 6.04 us -> none  [the longest x1 3.28 us: on_device(): state[:, :, :, 1:]]
    add x3 -> x0, other arithmetic: 6.04 us -> none  [the longest x1 5.4 us: on_device(): -(radial_u[None] * d_radial + (theta_u / radius)[None] * d_theta + axial_...]
    pallas_call x1, Pallas kernels: 33.6 us -> 39.6 us  [on_device(): pl.pallas_call(functools.partial(stencil_kernel, sectors, slabs), out_sha...]
    add x1 -> x0, local copies, waits for them, and re-layouts: 2.98 us -> none  [on_device(): return state + time_step * change]
    ppermute x2 -> x0, local copies, waits for them, and re-layouts: 2.17 us -> none  [the longest x1 1.09 us: with_halo(): lax.ppermute(lax.slice_in_dim(block, block.shape[dim] - width, None, axis...]
    div x1 -> x0, other arithmetic: 1.55 us -> none  [operators(): d_theta = (theta_plus - theta_minus) / (2.0 * step_angle)]
    mul x3 -> x0, other arithmetic: 1.25 us -> none  [the longest x1 1.23 us: on_device(): radial_u[None] * d_radial + (theta_u / radius)[None] * d_theta]
  transfers between devices with their start and end apart: 5 -> 0, of which waited for: 0 -> 0; matrix products, arithmetic and copies ran while one was open for 13% -> 0% of each run, Pallas kernels for 0% -> 0%
where the time goes in v2:
time: 43.9 us; the launch traced here: 43.8 us
  Pallas kernels  39.6 us (90%)
  local copies, waits for them, and re-layouts  4.19 us (10%)
    pallas_call x1, Pallas kernels, on_device(): pl.pallas_call(functools.partial(stencil_kernel, sectors, slabs), out_sha...  39.6 us
    unnamed x5, local copies, waits for them, and re-layouts  4.19 us

profile of v2, /device:TPU:1, one launch (start us, length us, event | category | flops | bytes accessed | tf_op | source)
XLA Modules:
  0.0 43.8 jit_solution(10199953552271297752)
XLA Ops:
  0.0 0.0 copy-start
  0.0 1.5 %copy-done = bf16[3,576,512]{2,1,0:T(8,128)(2,1)S(1)} copy-done((bf16[3,576,512]{2,1,0:T(8,128)(2,1)S(1)}, bf16[3,576,512]{2,1,0:T(8,128)(2,1)}, u32[]{:S(2)}) %copy-start) | copy-done | bytes 1769496
  1.5 0.0 copy-start.1
  1.5 1.2 %copy-done.1 = bf16[2,512,512]{2,1,0:T(8,128)(2,1)S(1)} copy-done((bf16[2,512,512]{2,1,0:T(8,128)(2,1)S(1)}, bf16[2,512,512]{2,1,0:T(8,128)(2,1)}, u32[]{:S(2)}) %copy-start.1) | copy-done | bytes 1048600
  2.7 39.6 %plume_section.1 = f32[5,16,16,512]{3,2,1,0:T(8,128)S(1)} custom-call(f32[5,16,16,512]{3,2,1,0:T(8,128)} %fields.1, bf16[2,512,512]{2,1,0:T(8,128)(2,1)S(1)} %copy-done.1, bf16[3,576,512]{2,1,0:T(8,128)(2,1)S(1)} %copy-done), custom_call_target="tpu_custom_call" | custom-call | tf_op jit(solution)/shard_map/plume_section/pallas_call | solution.py:438
  42.3 1.5 %copy.5 = f32[5,16,16,512]{3,2,1,0:T(8,128)} copy(f32[5,16,16,512]{3,2,1,0:T(8,128)S(1)} %plume_section.1) | data formatting | bytes 5242880
Async XLA Ops:
  0.0 1.5 %copy-start = (bf16[3,576,512]{2,1,0:T(8,128)(2,1)S(1)}, bf16[3,576,512]{2,1,0:T(8,128)(2,1)}, u32[]{:S(2)}) copy-start(bf16[3,576,512]{2,1,0:T(8,128)(2,1)} %constant.5.clone.inverse_hbm) | copy-start | bytes 5308420
  1.5 1.2 %copy-start.1 = (bf16[2,512,512]{2,1,0:T(8,128)(2,1)S(1)}, bf16[2,512,512]{2,1,0:T(8,128)(2,1)}, u32[]{:S(2)}) copy-start(bf16[2,512,512]{2,1,0:T(8,128)(2,1)} %constant.4.clone.forward_hbm) | copy-start | bytes 3145732

commit v3 on v2

--- a/solution.py
+++ b/solution.py
@@ -33,8 +33,8 @@
     return np.stack(out)
 
 
-def basis(theta, total):
-    mode = np.arange(MODES)
+def basis(theta, parity, total):
+    mode = np.arange(parity, MODES, 2)
     angle = (theta[..., None] * mode % total) * (2.0 * np.pi / total)
     return np.concatenate([np.cos(angle), np.sin(angle)], axis=-1)
 
@@ -42,18 +42,25 @@
 def transform_tables(sectors, theta_dev):
     total = sectors * theta_dev
     half = theta_dev // 2
-    sector = np.arange(sectors)[:, None] * theta_dev
-    mode = np.arange(MODES)
-    weight = np.concatenate([np.where(mode == 0, 1.0, 2.0), np.full(MODES, 2.0)]) / total
+    sector = np.arange(sectors // 2)[:, None] * theta_dev
     forward = []
     inverse = []
-    for side in range(2):
-        theta = (sector + side * half + np.arange(half)).reshape(-1)
-        forward.append((basis(theta, total) * weight).T)
-        first = sector + (half if side else -1)
-        theta = np.concatenate([(first + np.arange(half)).reshape(-1), (first + half).reshape(-1)])
-        inverse.append(basis(theta, total))
-    return split(np.concatenate(forward, axis=0), 2), split(np.concatenate(inverse, axis=1), 3)
+    for parity in range(2):
+        mode = np.arange(parity, MODES, 2)
+        weight = np.concatenate([np.where(mode == 0, 1.0, 2.0), np.full(MODES // 2, 2.0)]) / total
+        into = []
+        back = []
+        for side in range(2):
+            theta = (sector + side * half + np.arange(half)).reshape(-1)
+            into.append((basis(theta, parity, total) * weight).T)
+            first = sector + (half if side else -1)
+            theta = np.concatenate(
+                [(first + np.arange(half)).reshape(-1), (first + half).reshape(-1)]
+            )
+            back.append(basis(theta, parity, total))
+        forward.append(split(np.concatenate(into, axis=0), 2))
+        inverse.append(split(np.concatenate(back, axis=1), 3))
+    return np.stack(forward), np.stack(inverse)
 
 
 def stencil_kernel(
@@ -105,19 +112,38 @@
     load_inverse = pltpu.make_async_copy(inverse_hbm, inverse, load_sem.at[tiles + 1])
     load_inverse.start()
 
-    barrier = pltpu.get_barrier_semaphore()
-
-    def greet(i, carry):
-        pl.semaphore_signal(
-            barrier, inc=1, device_id={"az": (me + i) % sectors}, device_id_type=MESH
-        )
-        return carry
-
-    lax.fori_loop(1, sectors, greet, 0)
+    partner = (slab + slabs // 2) % slabs
     above = (slab + 1) % slabs
     below = (slab + slabs - 1) % slabs
+    ahead = (me + 1) % sectors
+    behind = (me + sectors - 1) % sectors
+    own_x = me // 16
+    own_y = me // 8 % 2
+    own_z = me % 8
+
+    def visit(call):
+        def one(i, carry):
+            step_x = (2 + (1 - 2 * (i // 16 % 2)) * ((i // 16 + 1) // 2)) % 4
+            rest = i % 16 // 2
+            step_z = 4 + (1 - 2 * (rest % 2)) * ((rest + 1) // 2)
+            peer = (own_x + step_x) % 4 * 16 + (own_y + i) % 2 * 8 + (own_z + step_z) % 8
+            call(peer)
+            return carry
+
+        lax.fori_loop(0, sectors, one, 0)
+
+    barrier = pltpu.get_barrier_semaphore()
+
+    def greet(peer):
+        pl.semaphore_signal(
+            barrier, inc=1, device_id={"az": peer, "ax": partner}, device_id_type=MESH
+        )
+
+    visit(greet)
     for neighbour in (above, below):
         pl.semaphore_signal(barrier, inc=1, device_id={"ax": neighbour}, device_id_type=MESH)
+    for neighbour in (ahead, behind):
+        pl.semaphore_signal(barrier, inc=1, device_id={"az": neighbour}, device_id_type=MESH)
 
     loads[0].wait()
     lane = lax.broadcasted_iota(jnp.int32, (half, LANES), 1)
@@ -140,29 +166,26 @@
         return carry
 
     lax.fori_loop(0, planes, pack, 0)
-    pl.semaphore_wait(barrier, sectors + 1)
+    pl.semaphore_wait(barrier, sectors + 4)
 
     def exchange(source, target, index):
-        def post(i, carry):
-            peer = (me + i) % sectors
+        def post(peer):
             pltpu.make_async_remote_copy(
                 src_ref=source.at[peer],
                 dst_ref=target.at[me],
                 send_sem=send_sem.at[index],
                 recv_sem=recv_sem.at[index],
-                device_id={"az": peer},
+                device_id={"az": peer, "ax": partner},
                 device_id_type=MESH,
             ).start()
-            return carry
-
-        lax.fori_loop(1, sectors, post, 0)
-        target[me] = source[me]
+
+        visit(post)
         return pltpu.make_async_remote_copy(
-            src_ref=source.at[pl.ds(0, sectors - 1)],
-            dst_ref=target.at[pl.ds(0, sectors - 1)],
+            src_ref=source,
+            dst_ref=target,
             send_sem=send_sem.at[index],
             recv_sem=recv_sem.at[index],
-            device_id={"az": (me + 1) % sectors},
+            device_id={"az": me, "ax": partner},
             device_id_type=MESH,
         )
 
@@ -199,7 +222,7 @@
 
     lax.fori_loop(0, tiles * FIELDS, collect, 0)
     edges = []
-    for side, peer in ((0, (me + sectors - 1) % sectors), (1, (me + 1) % sectors)):
+    for side, peer in ((0, behind), (1, ahead)):
         edges.append(
             pltpu.make_async_remote_copy(
                 src_ref=edge_send.at[side],
@@ -215,41 +238,55 @@
     load_forward.wait()
     load_inverse.wait()
     first_exchange.wait_recv()
-    values = recv1[...].reshape(sectors * half, LANES)
-    high = values.astype(jnp.bfloat16)
-    low = (values - high.astype(jnp.float32)).astype(jnp.bfloat16)
     dot = functools.partial(jnp.dot, preferred_element_type=jnp.float32)
-    spectra = dot(forward[0], high) + (dot(forward[0], low) + dot(forward[1], high))
-    row = lax.broadcasted_iota(jnp.int32, (2 * MODES, LANES), 0)
-    column = lax.broadcasted_iota(jnp.int32, (2 * MODES, LANES), 1)
-    spectra = jnp.where(column < HALF, spectra[: 2 * MODES], spectra[2 * MODES :])
-    spectra = spectra + pltpu.roll(spectra, HALF, 1)
+    pairs = sectors // 2
+    row = lax.broadcasted_iota(jnp.int32, (MODES, LANES), 0)
+    column = lax.broadcasted_iota(jnp.int32, (MODES, LANES), 1)
     slot = jnp.where(column < HALF, column, column - HALF)
     group = me % 4
     cycle = jnp.where(slot < NEAR, slot, slot - NEAR + QUARTER * group)
     cutoff = jnp.floor((355 * (2 * cycle + 1)).astype(jnp.float32) / 226.0 + 0.001)
-    mode = jnp.where(row < MODES, row, row - MODES)
-    kept = mode.astype(jnp.float32) <= jnp.minimum(cutoff, MODES - 1.0)
-    spectra = jnp.where(kept, spectra, 0.0)
-    parity = jnp.where(mode % 2 == 0, 1.0, -1.0)
+    cutoff = jnp.minimum(cutoff, MODES - 1.0)
     vector_sign = jnp.where(group < 2, -1.0, 1.0)
-    spectra = jnp.where(
-        slot == HALF - 1,
-        parity * vector_sign * pltpu.roll(spectra, HALF - 1, 1),
-        jnp.where(slot == HALF - 2, parity * pltpu.roll(spectra, HALF - 2 - NEAR, 1), spectra),
-    )
-    spectra = jnp.concatenate(
-        [jnp.where(column < HALF, spectra, 0.0), jnp.where(column < HALF, 0.0, spectra)], axis=0
-    )
-    high = spectra.astype(jnp.bfloat16)
-    rest = spectra - high.astype(jnp.float32)
-    medium = rest.astype(jnp.bfloat16)
-    low = (rest - medium.astype(jnp.float32)).astype(jnp.bfloat16)
-    smooth = dot(inverse[0], low) + dot(inverse[1], medium) + dot(inverse[2], high)
-    smooth = smooth + (dot(inverse[0], medium) + dot(inverse[1], high))
-    smooth = smooth + dot(inverse[0], high)
-    send2[:, 0:half, :] = smooth[: sectors * half].reshape(sectors, half, LANES)
-    extra[...] = smooth[sectors * half :]
+    smooth = []
+    for parity in range(2):
+        near_half = recv1[0:pairs].reshape(pairs * half, LANES)
+        far_half = recv1[pairs:].reshape(pairs * half, LANES)
+        values = near_half - far_half if parity else near_half + far_half
+        high = values.astype(jnp.bfloat16)
+        low = (values - high.astype(jnp.float32)).astype(jnp.bfloat16)
+        both = dot(forward[parity, 0], jnp.concatenate([high, low], axis=1))
+        spectra = both[:, :LANES] + (both[:, LANES:] + dot(forward[parity, 1], high))
+        spectra = jnp.where(column < HALF, spectra[:MODES], spectra[MODES:])
+        spectra = spectra + pltpu.roll(spectra, HALF, 1)
+        mode = 2 * jnp.where(row < MODES // 2, row, row - MODES // 2) + parity
+        spectra = jnp.where(mode.astype(jnp.float32) <= cutoff, spectra, 0.0)
+        sign = -1.0 if parity else 1.0
+        spectra = jnp.where(
+            slot == HALF - 1,
+            (sign * vector_sign) * pltpu.roll(spectra, HALF - 1, 1),
+            jnp.where(slot == HALF - 2, sign * pltpu.roll(spectra, HALF - 2 - NEAR, 1), spectra),
+        )
+        spectra = jnp.concatenate(
+            [jnp.where(column < HALF, spectra, 0.0), jnp.where(column < HALF, 0.0, spectra)],
+            axis=0,
+        )
+        high = spectra.astype(jnp.bfloat16)
+        rest = spectra - high.astype(jnp.float32)
+        medium = rest.astype(jnp.bfloat16)
+        low = (rest - medium.astype(jnp.float32)).astype(jnp.bfloat16)
+        wide = jnp.concatenate([high, medium], axis=1)
+        first = dot(inverse[parity, 0], wide)
+        second = dot(inverse[parity, 1], wide)
+        third = dot(inverse[parity, 0], low) + dot(inverse[parity, 2], high)
+        third = third + second[:, LANES:]
+        smooth.append(first[:, :LANES] + (first[:, LANES:] + second[:, :LANES] + third))
+    for side in range(2):
+        value = smooth[0] - smooth[1] if side else smooth[0] + smooth[1]
+        send2[side * pairs : (side + 1) * pairs, 0:half, :] = value[: pairs * half].reshape(
+            pairs, half, LANES
+        )
+        extra[side * pairs : (side + 1) * pairs, :] = value[pairs * half :]
 
     def last_rows(i, carry):
         for d in range(8):
@@ -328,12 +365,12 @@
 
     stores = []
 
-    def store(tile):
+    def store(tile, first_plane, count):
         stores.append(
             pltpu.make_async_copy(
-                result.at[tile],
-                advanced.at[:, :, :, pl.ds(tile * LANES, LANES)],
-                store_sem.at[tile],
+                result.at[tile, :, pl.ds(first_plane, count)],
+                advanced.at[:, pl.ds(first_plane, count), :, pl.ds(tile * LANES, LANES)],
+                store_sem.at[len(stores)],
             )
         )
         stores[-1].start()
@@ -345,7 +382,7 @@
             return carry
 
         lax.fori_loop(0, planes, far, 0)
-        store(tile)
+        store(tile, 0, planes)
 
     second_exchange.wait_recv()
 
@@ -413,12 +450,14 @@
         return carry
 
     lax.fori_loop(1, planes - 1, near, 0)
+    store(0, 1, planes - 2)
     for copy in near_planes:
         copy.wait_recv()
     close(0, 1)
     advance(0, 0)
+    store(0, 0, 1)
     advance(0, planes - 1)
-    store(0)
+    store(0, planes - 1, 1)
     first_exchange.wait_send()
     second_exchange.wait_send()
     for copy in edges + far_planes + near_planes:
@@ -454,7 +493,7 @@
             pltpu.VMEM((2, tiles, count, planes, LANES), jnp.float32),
             pltpu.VMEM((2, tiles, count, planes, LANES), jnp.float32),
             pltpu.SemaphoreType.DMA((tiles + 2,)),
-            pltpu.SemaphoreType.DMA((tiles,)),
+            pltpu.SemaphoreType.DMA((tiles + 2,)),
             pltpu.SemaphoreType.DMA((8,)),
             pltpu.SemaphoreType.DMA((8,)),
         ],
@@ -462,7 +501,11 @@
             collective_id=0, has_side_effects=True, vmem_limit_bytes=48 << 20
         ),
         name="plume_section",
-    )(fields, jnp.asarray(forward), jnp.asarray(inverse))
+    )(
+        pltpu.with_memory_space_constraint(fields, pltpu.HBM),
+        pltpu.with_memory_space_constraint(jnp.asarray(forward), pltpu.HBM),
+        pltpu.with_memory_space_constraint(jnp.asarray(inverse), pltpu.HBM),
+    )
 
 
 def solution(mesh):

time: 43.9 us -> 37.9 us (0.86)
  Pallas kernels: 39.6 us -> 36.3 us
  local copies, waits for them, and re-layouts: 4.19 us -> 1.49 us
    pallas_call x1, Pallas kernels: 39.6 us -> 36.3 us  [on_device(): pl.pallas_call(functools.partial(stencil_kernel, sectors, slabs), out_sha...]
    unnamed x5 -> x1, local copies, waits for them, and re-layouts: 4.19 us -> 1.49 us
where the time goes in v3:
time: 37.9 us; the launch traced here: 37.8 us
  Pallas kernels  36.3 us (96%)
  local copies, waits for them, and re-layouts  1.49 us (4%)
    pallas_call x1, Pallas kernels, on_device(): pl.pallas_call(functools.partial(stencil_kernel, sectors, slabs), out_sha...  36.3 us
    unnamed x1, local copies, waits for them, and re-layouts  1.49 us

profile of v3, /device:TPU:1, one launch (start us, length us, event | category | flops | bytes accessed | tf_op | source)
XLA Modules:
  0.0 37.8 jit_solution(2193245199931557905)
XLA Ops:
  0.0 36.3 %plume_section.1 = f32[5,16,16,512]{3,2,1,0:T(8,128)S(1)} custom-call(f32[5,16,16,512]{3,2,1,0:T(8,128)} %fields.1, bf16[2,2,256,256]{3,2,1,0:T(8,128)(2,1)} %constant.4.clone.forward_hbm, bf16[2,3,288,256]{3,2,1,0:T(8,128)(2,1)} %constant.5.clone.inverse_hbm), custom_call_target="tpu_custom_call" | custom-call | tf_op jit(solution)/shard_map/plume_section/pallas_call | solution.py:477
  36.4 1.5 %copy.5 = f32[5,16,16,512]{3,2,1,0:T(8,128)} copy(f32[5,16,16,512]{3,2,1,0:T(8,128)S(1)} %plume_section.1) | data formatting | bytes 5242880

commit v4 on v3

--- a/solution.py
+++ b/solution.py
@@ -15,6 +15,8 @@
 LANES = 128
 HALF = 64
 QUARTER = 10
+SPAN = 7
+ORDER = (0, 1, 3, 2)
 TOP = 8
 MESH = pl.DeviceIdType.MESH
 
@@ -53,10 +55,8 @@
         for side in range(2):
             theta = (sector + side * half + np.arange(half)).reshape(-1)
             into.append((basis(theta, parity, total) * weight).T)
-            first = sector + (half if side else -1)
-            theta = np.concatenate(
-                [(first + np.arange(half)).reshape(-1), (first + half).reshape(-1)]
-            )
+            edge = sector + (theta_dev if side else -1)
+            theta = np.concatenate([theta, edge.reshape(-1)])
             back.append(basis(theta, parity, total))
         forward.append(split(np.concatenate(into, axis=0), 2))
         inverse.append(split(np.concatenate(back, axis=1), 3))
@@ -80,6 +80,7 @@
     send2,
     recv2,
     extra,
+    ghost,
     edge_send,
     edge_recv,
     load_sem,
@@ -97,21 +98,6 @@
     middle = TOP + half
     step_angle = 2.0 * np.pi / (sectors * theta_dev)
 
-    loads = []
-    for tile in range(tiles):
-        loads.append(
-            pltpu.make_async_copy(
-                fields.at[:, :, :, pl.ds(tile * LANES, LANES)],
-                state.at[tile, :, pl.ds(1, planes), body, :],
-                load_sem.at[tile],
-            )
-        )
-        loads[-1].start()
-    load_forward = pltpu.make_async_copy(forward_hbm, forward, load_sem.at[tiles])
-    load_forward.start()
-    load_inverse = pltpu.make_async_copy(inverse_hbm, inverse, load_sem.at[tiles + 1])
-    load_inverse.start()
-
     partner = (slab + slabs // 2) % slabs
     above = (slab + 1) % slabs
     below = (slab + slabs - 1) % slabs
@@ -121,6 +107,16 @@
     own_y = me // 8 % 2
     own_z = me % 8
 
+    own_group = own_z // 2
+    own_plane = me // 8 * 2 + me % 2
+    served = partner
+    serves_below = (own_plane == 0) & (served > 0)
+    serves_above = (own_plane == planes - 1) & (served < slabs - 1)
+    serves_edge = serves_below | serves_above
+
+    def owner(k, f):
+        return k // 2 * 8 + 2 * f + k % 2
+
     def visit(call):
         def one(i, carry):
             step_x = (2 + (1 - 2 * (i // 16 % 2)) * ((i // 16 + 1) // 2)) % 4
@@ -145,6 +141,41 @@
     for neighbour in (ahead, behind):
         pl.semaphore_signal(barrier, inc=1, device_id={"az": neighbour}, device_id_type=MESH)
 
+    for f in range(4):
+
+        @pl.when(slab < slabs - 1)
+        def _():
+            pl.semaphore_signal(
+                barrier,
+                inc=1,
+                device_id={"az": owner(0, f), "ax": (slab + 1 + slabs // 2) % slabs},
+                device_id_type=MESH,
+            )
+
+        @pl.when(slab > 0)
+        def _():
+            pl.semaphore_signal(
+                barrier,
+                inc=1,
+                device_id={"az": owner(planes - 1, f), "ax": (slab + slabs // 2 - 1) % slabs},
+                device_id_type=MESH,
+            )
+
+    loads = []
+    for tile in range(tiles):
+        loads.append(
+            pltpu.make_async_copy(
+                fields.at[:, :, :, pl.ds(tile * LANES, LANES)],
+                state.at[tile, :, pl.ds(1, planes), body, :],
+                load_sem.at[tile],
+            )
+        )
+        loads[-1].start()
+    load_forward = pltpu.make_async_copy(forward_hbm, forward, load_sem.at[tiles])
+    load_forward.start()
+    load_inverse = pltpu.make_async_copy(inverse_hbm, inverse, load_sem.at[tiles + 1])
+    load_inverse.start()
+
     loads[0].wait()
     lane = lax.broadcasted_iota(jnp.int32, (half, LANES), 1)
     lane_row = lax.broadcasted_iota(jnp.int32, (1, LANES), 1)
@@ -162,34 +193,36 @@
                 state[0, f, k + 1, middle : middle + half, :],
                 pltpu.roll(tail1, shift, 1),
             )
-            send1[k * 4 + f] = jnp.where(lane < HALF, first, pltpu.roll(second, HALF, 1))
+            send1[owner(k, f)] = jnp.where(lane < HALF, first, pltpu.roll(second, HALF, 1))
         return carry
 
     lax.fori_loop(0, planes, pack, 0)
-    pl.semaphore_wait(barrier, sectors + 4)
-
-    def exchange(source, target, index):
+    pl.semaphore_wait(barrier, sectors + 4 + jnp.where(serves_edge, sectors, 0))
+
+    def exchange(source, target, index, arrival):
         def post(peer):
             pltpu.make_async_remote_copy(
                 src_ref=source.at[peer],
                 dst_ref=target.at[me],
                 send_sem=send_sem.at[index],
-                recv_sem=recv_sem.at[index],
+                recv_sem=recv_sem.at[arrival],
                 device_id={"az": peer, "ax": partner},
                 device_id_type=MESH,
             ).start()
 
         visit(post)
+
+    def whole(buffer, count, index, arrival):
         return pltpu.make_async_remote_copy(
-            src_ref=source,
-            dst_ref=target,
+            src_ref=buffer.at[pl.ds(0, count)],
+            dst_ref=buffer.at[pl.ds(0, count)],
             send_sem=send_sem.at[index],
-            recv_sem=recv_sem.at[index],
+            recv_sem=recv_sem.at[arrival],
             device_id={"az": me, "ax": partner},
             device_id_type=MESH,
         )
 
-    first_exchange = exchange(send1, recv1, 0)
+    exchange(send1, recv1, 0, 0)
 
     def plane_copy(first_tile, count, source, target, neighbour, index):
         return pltpu.make_async_remote_copy(
@@ -204,8 +237,8 @@
     for load in loads[1:]:
         load.wait()
     far_planes = [
-        plane_copy(1, tiles - 1, planes, 0, above, 2),
-        plane_copy(1, tiles - 1, 1, planes + 1, below, 3),
+        plane_copy(0, tiles, planes, 0, above, 2),
+        plane_copy(0, tiles, 1, planes + 1, below, 3),
     ]
     for copy in far_planes:
         copy.start()
@@ -237,13 +270,13 @@
 
     load_forward.wait()
     load_inverse.wait()
-    first_exchange.wait_recv()
+    whole(recv1, sectors, 0, 0).wait_recv()
     dot = functools.partial(jnp.dot, preferred_element_type=jnp.float32)
     pairs = sectors // 2
     row = lax.broadcasted_iota(jnp.int32, (MODES, LANES), 0)
     column = lax.broadcasted_iota(jnp.int32, (MODES, LANES), 1)
     slot = jnp.where(column < HALF, column, column - HALF)
-    group = me % 4
+    group = own_group
     cycle = jnp.where(slot < NEAR, slot, slot - NEAR + QUARTER * group)
     cutoff = jnp.floor((355 * (2 * cycle + 1)).astype(jnp.float32) / 226.0 + 0.001)
     cutoff = jnp.minimum(cutoff, MODES - 1.0)
@@ -283,18 +316,43 @@
         smooth.append(first[:, :LANES] + (first[:, LANES:] + second[:, :LANES] + third))
     for side in range(2):
         value = smooth[0] - smooth[1] if side else smooth[0] + smooth[1]
-        send2[side * pairs : (side + 1) * pairs, 0:half, :] = value[: pairs * half].reshape(
+        send2[side * pairs : (side + 1) * pairs] = value[: pairs * half].reshape(
             pairs, half, LANES
         )
-        extra[side * pairs : (side + 1) * pairs, :] = value[pairs * half :]
-
-    def last_rows(i, carry):
+        for i in range(half):
+            first_row = i * sectors + side * pairs
+            extra[first_row : first_row + pairs, :] = pltpu.roll(
+                value[pairs * half :], (NEAR + QUARTER - SPAN * i) % LANES, 1
+            )
+
+    slot8 = jnp.where(lane < HALF, lane, lane - HALF)
+    spare = (slot8 >= NEAR + QUARTER) & (slot8 < NEAR + QUARTER + SPAN)
+
+    def edge_lanes(i, carry):
         for d in range(8):
-            send2[i * 8 + d, half : half + 1, :] = extra[pl.ds(i * 8 + d, 1), :]
+            turned = extra[pl.ds(i * 8 + d, half, stride=sectors), :]
+            send2[i * 8 + d] = jnp.where(spare, turned, send2[i * 8 + d])
         return carry
 
-    lax.fori_loop(0, sectors // 8, last_rows, 0)
-    second_exchange = exchange(send2, recv2, 1)
+    lax.fori_loop(0, sectors // 8, edge_lanes, 0)
+    exchange(send2, recv2, 1, 8 + own_x)
+
+    @pl.when(serves_edge)
+    def _():
+        side = jnp.where(serves_below, 1, 0)
+        neighbour = served + 1 - 2 * side
+
+        def post(peer):
+            pltpu.make_async_remote_copy(
+                src_ref=send2.at[peer],
+                dst_ref=ghost.at[side, own_group],
+                send_sem=send_sem.at[6],
+                recv_sem=recv_sem.at[6 + side],
+                device_id={"az": peer, "ax": neighbour},
+                device_id_type=MESH,
+            ).start()
+
+        visit(post)
 
     for copy in edges + far_planes:
         copy.wait_recv()
@@ -321,7 +379,7 @@
                     for f in range(FIELDS):
                         state[tile, f, plane, body, :] = nothing
 
-    close(1, tiles)
+    close(0, tiles)
     lane_full = lax.broadcasted_iota(jnp.int32, (theta_dev, LANES), 1)
 
     def advance(tile, k):
@@ -384,83 +442,113 @@
         lax.fori_loop(0, planes, far, 0)
         store(tile, 0, planes)
 
-    second_exchange.wait_recv()
+    for copy in far_planes:
+        copy.wait_send()
+    sublane = lax.broadcasted_iota(jnp.int32, (half, LANES), 0)
+    diagonal = (slot8 >= SPAN * sublane) & (slot8 < SPAN * sublane + SPAN)
+    low_row = TOP - 1
+    high_row = TOP + theta_dev
+    is_near = lane < NEAR
+    is_near_row = lane_row < NEAR
 
     def unpack(k):
-        tail = [
-            state[0, 4, k + 1, TOP:middle, :],
-            state[0, 4, k + 1, middle : middle + half, :],
-            state[0, 4, k + 1, TOP - 1 : TOP, :],
-            state[0, 4, k + 1, TOP + theta_dev : TOP + theta_dev + 1, :],
-        ]
+        tail = state.at[0, 4, k + 1]
+        tail0 = tail[TOP:middle, :]
+        tail1 = tail[middle : middle + half, :]
+        tail2 = tail[low_row : low_row + 1, :]
+        tail3 = tail[high_row : high_row + 1, :]
         for f in range(4):
-            got0 = recv2[k * 4 + f, 1 : half + 1, :]
-            got1 = recv2[k * 4 + f, 0:half, :]
-            got2 = recv2[k * 4 + f, 0:1, :]
-            got3 = recv2[k * 4 + f, half : half + 1, :]
-            turned = pltpu.roll(got1, HALF, 1)
-            across[f, k, 0:half, :] = pltpu.roll(got0, HALF, 1)
-            across[f, k, half:, :] = got1
-            near = lane < NEAR
-            near_row = lane_row < NEAR
+            got = recv2[owner(k, f)]
+            turned = pltpu.roll(got, HALF, 1)
+            across[f, k, 0:half, :] = turned
+            across[f, k, half:, :] = got
+            rows = pltpu.roll(got, LANES - NEAR - QUARTER, 1, stride=SPAN, stride_axis=0)
+            rows = jnp.sum(jnp.where(diagonal, rows, 0.0), axis=0, keepdims=True)
             here = state.at[0, f, k + 1]
-            here[TOP:middle, :] = jnp.where(near, got0, here[TOP:middle, :])
+            here[TOP:middle, :] = jnp.where(is_near, got, here[TOP:middle, :])
             here[middle : middle + half, :] = jnp.where(
-                near, turned, here[middle : middle + half, :]
-            )
-            here[TOP - 1 : TOP, :] = jnp.where(near_row, got2, here[TOP - 1 : TOP, :])
-            here[TOP + theta_dev : TOP + theta_dev + 1, :] = jnp.where(
-                near_row,
-                pltpu.roll(got3, HALF, 1),
-                here[TOP + theta_dev : TOP + theta_dev + 1, :],
+                is_near, turned, here[middle : middle + half, :]
+            )
+            here[low_row : low_row + 1, :] = jnp.where(
+                is_near_row, rows, here[low_row : low_row + 1, :]
+            )
+            here[high_row : high_row + 1, :] = jnp.where(
+                is_near_row, pltpu.roll(rows, HALF, 1), here[high_row : high_row + 1, :]
             )
             shift = (QUARTER * f - NEAR) % LANES
             other = (shift + HALF) % LANES
             part = (lane >= QUARTER * f) & (lane < QUARTER * (f + 1))
             part_row = (lane_row >= QUARTER * f) & (lane_row < QUARTER * (f + 1))
-            tail[0] = jnp.where(part, pltpu.roll(got0, shift, 1), tail[0])
-            tail[1] = jnp.where(part, pltpu.roll(got1, other, 1), tail[1])
-            tail[2] = jnp.where(part_row, pltpu.roll(got2, shift, 1), tail[2])
-            tail[3] = jnp.where(part_row, pltpu.roll(got3, other, 1), tail[3])
+            tail0 = jnp.where(part, pltpu.roll(got, shift, 1), tail0)
+            tail1 = jnp.where(part, pltpu.roll(got, other, 1), tail1)
+            tail2 = jnp.where(part_row, pltpu.roll(rows, shift, 1), tail2)
+            tail3 = jnp.where(part_row, pltpu.roll(rows, other, 1), tail3)
             if f == 0:
-                across[4, k, 0:half, :] = pltpu.roll(got0, HALF + 1, 1)
-                across[4, k, half:, :] = pltpu.roll(got1, 1, 1)
-        state[0, 4, k + 1, TOP:middle, :] = tail[0]
-        state[0, 4, k + 1, middle : middle + half, :] = tail[1]
-        state[0, 4, k + 1, TOP - 1 : TOP, :] = tail[2]
-        state[0, 4, k + 1, TOP + theta_dev : TOP + theta_dev + 1, :] = tail[3]
-
-    unpack(0)
-    unpack(planes - 1)
-    near_planes = [
-        plane_copy(0, 1, planes, 0, above, 6),
-        plane_copy(0, 1, 1, planes + 1, below, 7),
-    ]
-    for copy in near_planes:
-        copy.start()
-
-    def unpack_inner(k, carry):
-        unpack(k)
+                across[4, k, 0:half, :] = pltpu.roll(got, HALF + 1, 1)
+                across[4, k, half:, :] = pltpu.roll(got, 1, 1)
+        tail[TOP:middle, :] = tail0
+        tail[middle : middle + half, :] = tail1
+        tail[low_row : low_row + 1, :] = tail2
+        tail[high_row : high_row + 1, :] = tail3
+
+    def unpack_ghost(side, plane):
+        tail = state.at[0, 4, plane]
+        tail0 = tail[TOP:middle, :]
+        tail1 = tail[middle : middle + half, :]
+        for f in range(4):
+            got = ghost[side, f]
+            here = state.at[0, f, plane]
+            here[TOP:middle, :] = jnp.where(is_near, got, here[TOP:middle, :])
+            here[middle : middle + half, :] = jnp.where(
+                is_near, pltpu.roll(got, HALF, 1), here[middle : middle + half, :]
+            )
+            shift = (QUARTER * f - NEAR) % LANES
+            part = (lane >= QUARTER * f) & (lane < QUARTER * (f + 1))
+            tail0 = jnp.where(part, pltpu.roll(got, shift, 1), tail0)
+            tail1 = jnp.where(part, pltpu.roll(got, (shift + HALF) % LANES, 1), tail1)
+        tail[TOP:middle, :] = tail0
+        tail[middle : middle + half, :] = tail1
+
+    columns = sectors // 16
+    width = planes // columns
+
+    for step in ORDER:
+        group_x = (own_x + step) % columns
+        whole(recv2, 16, 1, 8 + group_x).wait_recv()
+
+        def unpack_one(i, carry):
+            unpack(group_x * width + i)
+            return carry
+
+        lax.fori_loop(0, width, unpack_one, 0)
+
+        def inside(i, carry):
+            advance(0, group_x * width + i)
+            return carry
+
+        lax.fori_loop(1, width - 1, inside, 0)
+    for side, plane, edge in ((0, 0, 0), (1, planes + 1, slabs - 1)):
+
+        @pl.when(slab != edge)
+        def _():
+            whole(ghost.at[side], 4, 6, 6 + side).wait_recv()
+            unpack_ghost(side, plane)
+
+    def border(i, carry):
+        advance(0, i * width)
+        advance(0, i * width + width - 1)
         return carry
 
-    lax.fori_loop(1, planes - 1, unpack_inner, 0)
-
-    def near(k, carry):
-        advance(0, k)
-        return carry
-
-    lax.fori_loop(1, planes - 1, near, 0)
-    store(0, 1, planes - 2)
-    for copy in near_planes:
-        copy.wait_recv()
-    close(0, 1)
-    advance(0, 0)
-    store(0, 0, 1)
-    advance(0, planes - 1)
-    store(0, planes - 1, 1)
-    first_exchange.wait_send()
-    second_exchange.wait_send()
-    for copy in edges + far_planes + near_planes:
+    lax.fori_loop(0, columns, border, 0)
+    store(0, 0, planes)
+    whole(send1, sectors, 0, 0).wait_send()
+    whole(send2, sectors, 1, 0).wait_send()
+
+    @pl.when(serves_edge)
+    def _():
+        whole(send2, sectors, 6, 0).wait_send()
+
+    for copy in edges:
         copy.wait_send()
     for copy in stores:
         copy.wait()
@@ -487,15 +575,16 @@
             pltpu.VMEM(inverse.shape, jnp.bfloat16),
             pltpu.VMEM((sectors, half, LANES), jnp.float32),
             pltpu.VMEM((sectors, half, LANES), jnp.float32),
-            pltpu.VMEM((sectors, half + 1, LANES), jnp.float32),
-            pltpu.VMEM((sectors, half + 1, LANES), jnp.float32),
-            pltpu.VMEM((sectors, LANES), jnp.float32),
+            pltpu.VMEM((sectors, half, LANES), jnp.float32),
+            pltpu.VMEM((sectors, half, LANES), jnp.float32),
+            pltpu.VMEM((sectors * half, LANES), jnp.float32),
+            pltpu.VMEM((2, 4, half, LANES), jnp.float32),
             pltpu.VMEM((2, tiles, count, planes, LANES), jnp.float32),
             pltpu.VMEM((2, tiles, count, planes, LANES), jnp.float32),
             pltpu.SemaphoreType.DMA((tiles + 2,)),
             pltpu.SemaphoreType.DMA((tiles + 2,)),
             pltpu.SemaphoreType.DMA((8,)),
-            pltpu.SemaphoreType.DMA((8,)),
+            pltpu.SemaphoreType.DMA((12,)),
         ],
         compiler_params=pltpu.CompilerParams(
             collective_id=0, has_side_effects=True, vmem_limit_bytes=48 << 20

time: 37.9 us -> 41.9 us (1.11)
  Pallas kernels: 36.3 us -> 40.3 us
    pallas_call x1, Pallas kernels: 36.3 us -> 40.3 us  [on_device(): pl.pallas_call(functools.partial(stencil_kernel, sectors, slabs), out_sha...]
where the time goes in v4:
time: 41.9 us; the launch traced here: 41.8 us
  Pallas kernels  40.3 us (96%)
  local copies, waits for them, and re-layouts  1.49 us (4%)
    pallas_call x1, Pallas kernels, on_device(): pl.pallas_call(functools.partial(stencil_kernel, sectors, slabs), out_sha...  40.3 us
    unnamed x1, local copies, waits for them, and re-layouts  1.49 us

profile of v4, /device:TPU:1, one launch (start us, length us, event | category | flops | bytes accessed | tf_op | source)
XLA Modules:
  0.0 41.8 jit_solution(9546291487517543540)
XLA Ops:
  0.0 40.3 %plume_section.1 = f32[5,16,16,512]{3,2,1,0:T(8,128)S(1)} custom-call(f32[5,16,16,512]{3,2,1,0:T(8,128)} %fields.1, bf16[2,2,256,256]{3,2,1,0:T(8,128)(2,1)} %constant.4.clone.forward_hbm, bf16[2,3,288,256]{3,2,1,0:T(8,128)(2,1)} %constant.5.clone.inverse_hbm), custom_call_target="tpu_custom_call" | custom-call | tf_op jit(solution)/shard_map/plume_section/pallas_call | solution.py:565
  40.3 1.5 %copy.5 = f32[5,16,16,512]{3,2,1,0:T(8,128)} copy(f32[5,16,16,512]{3,2,1,0:T(8,128)S(1)} %plume_section.1) | data formatting | bytes 5242880

commit v5 on v3

--- a/solution.py
+++ b/solution.py
@@ -15,6 +15,9 @@
 LANES = 128
 HALF = 64
 QUARTER = 10
+SPAN = 7
+WIDE = 2
+WIDE2 = 2
 TOP = 8
 MESH = pl.DeviceIdType.MESH
 
@@ -53,10 +56,8 @@
         for side in range(2):
             theta = (sector + side * half + np.arange(half)).reshape(-1)
             into.append((basis(theta, parity, total) * weight).T)
-            first = sector + (half if side else -1)
-            theta = np.concatenate(
-                [(first + np.arange(half)).reshape(-1), (first + half).reshape(-1)]
-            )
+            edge = sector + (theta_dev if side else -1)
+            theta = np.concatenate([theta, edge.reshape(-1)])
             back.append(basis(theta, parity, total))
         forward.append(split(np.concatenate(into, axis=0), 2))
         inverse.append(split(np.concatenate(back, axis=1), 3))
@@ -121,16 +122,22 @@
     own_y = me // 8 % 2
     own_z = me % 8
 
+    own_group = own_z // 2
+    own_plane = me // 8 * 2 + me % 2
+    owns_edge = (own_plane == 0) | (own_plane == planes - 1)
+
+    def owner(k, f):
+        return k // 2 * 8 + 2 * f + k % 2
+
+    around_x = [(own_x + step) % 4 * 16 for step in range(4)]
+    around_y = [(own_y + step) % 2 * 8 for step in range(2)]
+    around_z = [(own_z + step) % 8 for step in range(8)]
+
     def visit(call):
-        def one(i, carry):
-            step_x = (2 + (1 - 2 * (i // 16 % 2)) * ((i // 16 + 1) // 2)) % 4
-            rest = i % 16 // 2
-            step_z = 4 + (1 - 2 * (rest % 2)) * ((rest + 1) // 2)
-            peer = (own_x + step_x) % 4 * 16 + (own_y + i) % 2 * 8 + (own_z + step_z) % 8
-            call(peer)
-            return carry
-
-        lax.fori_loop(0, sectors, one, 0)
+        for step_x in (2, 1, 3, 0):
+            for step_z in (4, 3, 5, 2, 6, 1, 7, 0):
+                for step_y in range(2):
+                    call(around_x[step_x] + around_y[step_y] + around_z[step_z])
 
     barrier = pltpu.get_barrier_semaphore()
 
@@ -162,34 +169,36 @@
                 state[0, f, k + 1, middle : middle + half, :],
                 pltpu.roll(tail1, shift, 1),
             )
-            send1[k * 4 + f] = jnp.where(lane < HALF, first, pltpu.roll(second, HALF, 1))
+            send1[owner(k, f)] = jnp.where(lane < HALF, first, pltpu.roll(second, HALF, 1))
         return carry
 
     lax.fori_loop(0, planes, pack, 0)
     pl.semaphore_wait(barrier, sectors + 4)
 
-    def exchange(source, target, index):
+    def exchange(source, target, index, arrival):
         def post(peer):
             pltpu.make_async_remote_copy(
                 src_ref=source.at[peer],
                 dst_ref=target.at[me],
                 send_sem=send_sem.at[index],
-                recv_sem=recv_sem.at[index],
+                recv_sem=recv_sem.at[arrival],
                 device_id={"az": peer, "ax": partner},
                 device_id_type=MESH,
             ).start()
 
         visit(post)
+
+    def whole(buffer, count, index, arrival):
         return pltpu.make_async_remote_copy(
-            src_ref=source,
-            dst_ref=target,
+            src_ref=buffer.at[pl.ds(0, count)],
+            dst_ref=buffer.at[pl.ds(0, count)],
             send_sem=send_sem.at[index],
-            recv_sem=recv_sem.at[index],
+            recv_sem=recv_sem.at[arrival],
             device_id={"az": me, "ax": partner},
             device_id_type=MESH,
         )
 
-    first_exchange = exchange(send1, recv1, 0)
+    exchange(send1, recv1, 0, 0)
 
     def plane_copy(first_tile, count, source, target, neighbour, index):
         return pltpu.make_async_remote_copy(
@@ -237,13 +246,13 @@
 
     load_forward.wait()
     load_inverse.wait()
-    first_exchange.wait_recv()
+    whole(recv1, sectors, 0, 0).wait_recv()
     dot = functools.partial(jnp.dot, preferred_element_type=jnp.float32)
     pairs = sectors // 2
     row = lax.broadcasted_iota(jnp.int32, (MODES, LANES), 0)
     column = lax.broadcasted_iota(jnp.int32, (MODES, LANES), 1)
     slot = jnp.where(column < HALF, column, column - HALF)
-    group = me % 4
+    group = own_group
     cycle = jnp.where(slot < NEAR, slot, slot - NEAR + QUARTER * group)
     cutoff = jnp.floor((355 * (2 * cycle + 1)).astype(jnp.float32) / 226.0 + 0.001)
     cutoff = jnp.minimum(cutoff, MODES - 1.0)
@@ -283,18 +292,26 @@
         smooth.append(first[:, :LANES] + (first[:, LANES:] + second[:, :LANES] + third))
     for side in range(2):
         value = smooth[0] - smooth[1] if side else smooth[0] + smooth[1]
-        send2[side * pairs : (side + 1) * pairs, 0:half, :] = value[: pairs * half].reshape(
+        send2[side * pairs : (side + 1) * pairs] = value[: pairs * half].reshape(
             pairs, half, LANES
         )
-        extra[side * pairs : (side + 1) * pairs, :] = value[pairs * half :]
-
-    def last_rows(i, carry):
+        for i in range(half):
+            first_row = i * sectors + side * pairs
+            extra[first_row : first_row + pairs, :] = pltpu.roll(
+                value[pairs * half :], (NEAR + QUARTER - SPAN * i) % LANES, 1
+            )
+
+    slot8 = jnp.where(lane < HALF, lane, lane - HALF)
+    spare = (slot8 >= NEAR + QUARTER) & (slot8 < NEAR + QUARTER + SPAN)
+
+    def edge_lanes(i, carry):
         for d in range(8):
-            send2[i * 8 + d, half : half + 1, :] = extra[pl.ds(i * 8 + d, 1), :]
+            turned = extra[pl.ds(i * 8 + d, half, stride=sectors), :]
+            send2[i * 8 + d] = jnp.where(spare, turned, send2[i * 8 + d])
         return carry
 
-    lax.fori_loop(0, sectors // 8, last_rows, 0)
-    second_exchange = exchange(send2, recv2, 1)
+    lax.fori_loop(0, sectors // 8, edge_lanes, 0)
+    exchange(send2, recv2, 1, jnp.where(owns_edge, 8, 1))
 
     for copy in edges + far_planes:
         copy.wait_recv()
@@ -384,82 +401,89 @@
         lax.fori_loop(0, planes, far, 0)
         store(tile, 0, planes)
 
-    second_exchange.wait_recv()
-
-    def unpack(k):
-        tail = [
-            state[0, 4, k + 1, TOP:middle, :],
-            state[0, 4, k + 1, middle : middle + half, :],
-            state[0, 4, k + 1, TOP - 1 : TOP, :],
-            state[0, 4, k + 1, TOP + theta_dev : TOP + theta_dev + 1, :],
-        ]
-        for f in range(4):
-            got0 = recv2[k * 4 + f, 1 : half + 1, :]
-            got1 = recv2[k * 4 + f, 0:half, :]
-            got2 = recv2[k * 4 + f, 0:1, :]
-            got3 = recv2[k * 4 + f, half : half + 1, :]
-            turned = pltpu.roll(got1, HALF, 1)
-            across[f, k, 0:half, :] = pltpu.roll(got0, HALF, 1)
-            across[f, k, half:, :] = got1
-            near = lane < NEAR
-            near_row = lane_row < NEAR
-            here = state.at[0, f, k + 1]
-            here[TOP:middle, :] = jnp.where(near, got0, here[TOP:middle, :])
-            here[middle : middle + half, :] = jnp.where(
-                near, turned, here[middle : middle + half, :]
-            )
-            here[TOP - 1 : TOP, :] = jnp.where(near_row, got2, here[TOP - 1 : TOP, :])
-            here[TOP + theta_dev : TOP + theta_dev + 1, :] = jnp.where(
-                near_row,
-                pltpu.roll(got3, HALF, 1),
-                here[TOP + theta_dev : TOP + theta_dev + 1, :],
-            )
-            shift = (QUARTER * f - NEAR) % LANES
-            other = (shift + HALF) % LANES
-            part = (lane >= QUARTER * f) & (lane < QUARTER * (f + 1))
-            part_row = (lane_row >= QUARTER * f) & (lane_row < QUARTER * (f + 1))
-            tail[0] = jnp.where(part, pltpu.roll(got0, shift, 1), tail[0])
-            tail[1] = jnp.where(part, pltpu.roll(got1, other, 1), tail[1])
-            tail[2] = jnp.where(part_row, pltpu.roll(got2, shift, 1), tail[2])
-            tail[3] = jnp.where(part_row, pltpu.roll(got3, other, 1), tail[3])
-            if f == 0:
-                across[4, k, 0:half, :] = pltpu.roll(got0, HALF + 1, 1)
-                across[4, k, half:, :] = pltpu.roll(got1, 1, 1)
-        state[0, 4, k + 1, TOP:middle, :] = tail[0]
-        state[0, 4, k + 1, middle : middle + half, :] = tail[1]
-        state[0, 4, k + 1, TOP - 1 : TOP, :] = tail[2]
-        state[0, 4, k + 1, TOP + theta_dev : TOP + theta_dev + 1, :] = tail[3]
-
-    unpack(0)
-    unpack(planes - 1)
+    sublane = lax.broadcasted_iota(jnp.int32, (half, LANES), 0)
+    diagonal = (slot8 >= SPAN * sublane) & (slot8 < SPAN * sublane + SPAN)
+    low_row = TOP - 1
+    high_row = TOP + theta_dev
+    is_near = lane < NEAR
+    is_near_row = lane_row < NEAR
+
+    def unpack(plane_list):
+        updates = []
+        for k in plane_list:
+            tail = [
+                state[0, 4, k + 1, TOP:middle, :],
+                state[0, 4, k + 1, middle : middle + half, :],
+                state[0, 4, k + 1, low_row : low_row + 1, :],
+                state[0, 4, k + 1, high_row : high_row + 1, :],
+            ]
+            for f in range(4):
+                got = recv2[owner(k, f)]
+                turned = pltpu.roll(got, HALF, 1)
+                rows = pltpu.roll(got, LANES - NEAR - QUARTER, 1, stride=SPAN, stride_axis=0)
+                rows = jnp.sum(jnp.where(diagonal, rows, 0.0), axis=0, keepdims=True)
+                parts = [
+                    jnp.where(is_near, got, state[0, f, k + 1, TOP:middle, :]),
+                    jnp.where(is_near, turned, state[0, f, k + 1, middle : middle + half, :]),
+                    jnp.where(is_near_row, rows, state[0, f, k + 1, low_row : low_row + 1, :]),
+                    jnp.where(
+                        is_near_row,
+                        pltpu.roll(rows, HALF, 1),
+                        state[0, f, k + 1, high_row : high_row + 1, :],
+                    ),
+                ]
+                updates.append((f, k, parts, turned, got))
+                shift = (QUARTER * f - NEAR) % LANES
+                other = (shift + HALF) % LANES
+                part = (lane >= QUARTER * f) & (lane < QUARTER * (f + 1))
+                part_row = (lane_row >= QUARTER * f) & (lane_row < QUARTER * (f + 1))
+                tail[0] = jnp.where(part, pltpu.roll(got, shift, 1), tail[0])
+                tail[1] = jnp.where(part, pltpu.roll(got, other, 1), tail[1])
+                tail[2] = jnp.where(part_row, pltpu.roll(rows, shift, 1), tail[2])
+                tail[3] = jnp.where(part_row, pltpu.roll(rows, other, 1), tail[3])
+                if f == 0:
+                    opposite = (pltpu.roll(got, HALF + 1, 1), pltpu.roll(got, 1, 1))
+            updates.append((4, k, tail, *opposite))
+        for f, k, parts, first, second in updates:
+            state[0, f, k + 1, TOP:middle, :] = parts[0]
+            state[0, f, k + 1, middle : middle + half, :] = parts[1]
+            state[0, f, k + 1, low_row : low_row + 1, :] = parts[2]
+            state[0, f, k + 1, high_row : high_row + 1, :] = parts[3]
+            across[f, k, 0:half, :] = first
+            across[f, k, half:, :] = second
+
+    whole(recv2, 8, 1, 8).wait_recv()
+    unpack([0, planes - 1])
     near_planes = [
         plane_copy(0, 1, planes, 0, above, 6),
         plane_copy(0, 1, 1, planes + 1, below, 7),
     ]
     for copy in near_planes:
         copy.start()
-
-    def unpack_inner(k, carry):
-        unpack(k)
+    whole(recv2, sectors - 8, 1, 1).wait_recv()
+
+    def unpack_inner(i, carry):
+        unpack([1 + i * WIDE + step for step in range(WIDE)])
         return carry
 
-    lax.fori_loop(1, planes - 1, unpack_inner, 0)
-
-    def near(k, carry):
-        advance(0, k)
+    lax.fori_loop(0, (planes - 2) // WIDE, unpack_inner, 0)
+
+    def near(i, carry):
+        for step in range(WIDE2):
+            advance(0, 1 + i * WIDE2 + step)
         return carry
 
-    lax.fori_loop(1, planes - 1, near, 0)
+    lax.fori_loop(0, (planes - 2) // WIDE2, near, 0)
     store(0, 1, planes - 2)
     for copy in near_planes:
         copy.wait_recv()
     close(0, 1)
     advance(0, 0)
+    advance(0, planes - 1)
     store(0, 0, 1)
-    advance(0, planes - 1)
     store(0, planes - 1, 1)
-    first_exchange.wait_send()
-    second_exchange.wait_send()
+    whole(send1, sectors, 0, 0).wait_send()
+    whole(send2, sectors, 1, 1).wait_send()
     for copy in edges + far_planes + near_planes:
         copy.wait_send()
     for copy in stores:
@@ -487,15 +511,15 @@
             pltpu.VMEM(inverse.shape, jnp.bfloat16),
             pltpu.VMEM((sectors, half, LANES), jnp.float32),
             pltpu.VMEM((sectors, half, LANES), jnp.float32),
-            pltpu.VMEM((sectors, half + 1, LANES), jnp.float32),
-            pltpu.VMEM((sectors, half + 1, LANES), jnp.float32),
-            pltpu.VMEM((sectors, LANES), jnp.float32),
+            pltpu.VMEM((sectors, half, LANES), jnp.float32),
+            pltpu.VMEM((sectors, half, LANES), jnp.float32),
+            pltpu.VMEM((sectors * half, LANES), jnp.float32),
             pltpu.VMEM((2, tiles, count, planes, LANES), jnp.float32),
             pltpu.VMEM((2, tiles, count, planes, LANES), jnp.float32),
             pltpu.SemaphoreType.DMA((tiles + 2,)),
             pltpu.SemaphoreType.DMA((tiles + 2,)),
             pltpu.SemaphoreType.DMA((8,)),
-            pltpu.SemaphoreType.DMA((8,)),
+            pltpu.SemaphoreType.DMA((9,)),
         ],
         compiler_params=pltpu.CompilerParams(
             collective_id=0, has_side_effects=True, vmem_limit_bytes=48 << 20

time: 37.9 us -> 35.3 us (0.931)
  Pallas kernels: 36.3 us -> 33.8 us
    pallas_call x1, Pallas kernels: 36.3 us -> 33.8 us  [on_device(): pl.pallas_call(functools.partial(stencil_kernel, sectors, slabs), out_sha...]
where the time goes in v5:
time: 35.3 us
  Pallas kernels  33.8 us (96%)
  local copies, waits for them, and re-layouts  1.49 us (4%)
    pallas_call x1, Pallas kernels, on_device(): pl.pallas_call(functools.partial(stencil_kernel, sectors, slabs), out_sha...  33.8 us
    unnamed x1, local copies, waits for them, and re-layouts  1.49 us

profile of v5, /device:TPU:1, one launch (start us, length us, event | category | flops | bytes accessed | tf_op | source)
XLA Modules:
  0.0 35.3 jit_solution(3365836788855911362)
XLA Ops:
  0.0 33.8 %plume_section.1 = f32[5,16,16,512]{3,2,1,0:T(8,128)S(1)} custom-call(f32[5,16,16,512]{3,2,1,0:T(8,128)} %fields.1, bf16[2,2,256,256]{3,2,1,0:T(8,128)(2,1)} %constant.4.clone.forward_hbm, bf16[2,3,288,256]{3,2,1,0:T(8,128)(2,1)} %constant.5.clone.inverse_hbm), custom_call_target="tpu_custom_call" | custom-call | tf_op jit(solution)/shard_map/plume_section/pallas_call | solution.py:501
  33.8 1.5 %copy.5 = f32[5,16,16,512]{3,2,1,0:T(8,128)} copy(f32[5,16,16,512]{3,2,1,0:T(8,128)S(1)} %plume_section.1) | data formatting | bytes 5242880

commit v6 on v5

--- a/solution.py
+++ b/solution.py
@@ -81,6 +81,7 @@
     send2,
     recv2,
     extra,
+    ghost,
     edge_send,
     edge_recv,
     load_sem,
@@ -135,7 +136,7 @@
 
     def visit(call):
         for step_x in (2, 1, 3, 0):
-            for step_z in (4, 3, 5, 2, 6, 1, 7, 0):
+            for step_z in (4, 0, 3, 1, 5, 7, 2, 6):
                 for step_y in range(2):
                     call(around_x[step_x] + around_y[step_y] + around_z[step_z])
 
@@ -213,8 +214,8 @@
     for load in loads[1:]:
         load.wait()
     far_planes = [
-        plane_copy(1, tiles - 1, planes, 0, above, 2),
-        plane_copy(1, tiles - 1, 1, planes + 1, below, 3),
+        plane_copy(0, tiles, planes, 0, above, 2),
+        plane_copy(0, tiles, 1, planes + 1, below, 3),
     ]
     for copy in far_planes:
         copy.start()
@@ -452,14 +453,45 @@
             across[f, k, 0:half, :] = first
             across[f, k, half:, :] = second
 
+    for copy in far_planes:
+        copy.wait_send()
+
+    def unpack_ghosts():
+        updates = []
+        for side, plane, edge in ((0, 0, 0), (1, planes + 1, slabs - 1)):
+            inside = slab != edge
+            tail0 = state[0, 4, plane, TOP:middle, :]
+            tail1 = state[0, 4, plane, middle : middle + half, :]
+            for f in range(4):
+                got = ghost[side, f]
+                part0 = jnp.where(is_near, got, state[0, f, plane, TOP:middle, :])
+                part1 = jnp.where(
+                    is_near,
+                    pltpu.roll(got, HALF, 1),
+                    state[0, f, plane, middle : middle + half, :],
+                )
+                updates.append((f, plane, inside, part0, part1))
+                shift = (QUARTER * f - NEAR) % LANES
+                part = (lane >= QUARTER * f) & (lane < QUARTER * (f + 1))
+                tail0 = jnp.where(part, pltpu.roll(got, shift, 1), tail0)
+                tail1 = jnp.where(part, pltpu.roll(got, (shift + HALF) % LANES, 1), tail1)
+            updates.append((4, plane, inside, tail0, tail1))
+        for f, plane, inside, part0, part1 in updates:
+            state[0, f, plane, TOP:middle, :] = jnp.where(inside, part0, 0.0)
+            state[0, f, plane, middle : middle + half, :] = jnp.where(inside, part1, 0.0)
+
     whole(recv2, 8, 1, 8).wait_recv()
+    for f in range(4):
+        for side, plane, neighbour in ((0, planes - 1, above), (1, 0, below)):
+            pltpu.make_async_remote_copy(
+                src_ref=recv2.at[owner(plane, f)],
+                dst_ref=ghost.at[side, f],
+                send_sem=send_sem.at[6 + side],
+                recv_sem=recv_sem.at[6 + side],
+                device_id={"ax": neighbour},
+                device_id_type=MESH,
+            ).start()
     unpack([0, planes - 1])
-    near_planes = [
-        plane_copy(0, 1, planes, 0, above, 6),
-        plane_copy(0, 1, 1, planes + 1, below, 7),
-    ]
-    for copy in near_planes:
-        copy.start()
     whole(recv2, sectors - 8, 1, 1).wait_recv()
 
     def unpack_inner(i, carry):
@@ -475,16 +507,18 @@
 
     lax.fori_loop(0, (planes - 2) // WIDE2, near, 0)
     store(0, 1, planes - 2)
-    for copy in near_planes:
-        copy.wait_recv()
-    close(0, 1)
+    for side in range(2):
+        whole(ghost.at[side], 4, 6 + side, 6 + side).wait_recv()
+    unpack_ghosts()
     advance(0, 0)
     advance(0, planes - 1)
     store(0, 0, 1)
     store(0, planes - 1, 1)
     whole(send1, sectors, 0, 0).wait_send()
     whole(send2, sectors, 1, 1).wait_send()
-    for copy in edges + far_planes + near_planes:
+    for side in range(2):
+        whole(ghost.at[side], 4, 6 + side, 6 + side).wait_send()
+    for copy in edges:
         copy.wait_send()
     for copy in stores:
         copy.wait()
@@ -514,6 +548,7 @@
             pltpu.VMEM((sectors, half, LANES), jnp.float32),
             pltpu.VMEM((sectors, half, LANES), jnp.float32),
             pltpu.VMEM((sectors * half, LANES), jnp.float32),
+            pltpu.VMEM((2, 4, half, LANES), jnp.float32),
             pltpu.VMEM((2, tiles, count, planes, LANES), jnp.float32),
             pltpu.VMEM((2, tiles, count, planes, LANES), jnp.float32),
             pltpu.SemaphoreType.DMA((tiles + 2,)),

time: 35.3 us -> 34.9 us (0.989)
  Pallas kernels: 33.8 us -> 33.3 us
    pallas_call x1, Pallas kernels: 33.8 us -> 33.3 us  [on_device(): pl.pallas_call(functools.partial(stencil_kernel, sectors, slabs), out_sha...]
where the time goes in v6:
time: 34.9 us; the launch traced here: 34.8 us
  Pallas kernels  33.3 us (95%)
  local copies, waits for them, and re-layouts  1.49 us (4%)
    pallas_call x1, Pallas kernels, on_device(): pl.pallas_call(functools.partial(stencil_kernel, sectors, slabs), out_sha...  33.3 us
    unnamed x1, local copies, waits for them, and re-layouts  1.49 us

profile of v6, /device:TPU:1, one launch (start us, length us, event | category | flops | bytes accessed | tf_op | source)
XLA Modules:
  0.0 34.8 jit_solution(1296542298172067931)
XLA Ops:
  0.0 33.3 %plume_section.1 = f32[5,16,16,512]{3,2,1,0:T(8,128)S(1)} custom-call(f32[5,16,16,512]{3,2,1,0:T(8,128)} %fields.1, bf16[2,2,256,256]{3,2,1,0:T(8,128)(2,1)} %constant.4.clone.forward_hbm, bf16[2,3,288,256]{3,2,1,0:T(8,128)(2,1)} %constant.5.clone.inverse_hbm), custom_call_target="tpu_custom_call" | custom-call | tf_op jit(solution)/shard_map/plume_section/pallas_call | solution.py:535
  33.3 1.5 %copy.5 = f32[5,16,16,512]{3,2,1,0:T(8,128)} copy(f32[5,16,16,512]{3,2,1,0:T(8,128)S(1)} %plume_section.1) | data formatting | bytes 5242880

commit v7 on v6

--- a/solution.py
+++ b/solution.py
@@ -16,8 +16,6 @@
 HALF = 64
 QUARTER = 10
 SPAN = 7
-WIDE = 2
-WIDE2 = 2
 TOP = 8
 MESH = pl.DeviceIdType.MESH
 
@@ -341,6 +339,12 @@
 
     close(1, tiles)
     lane_full = lax.broadcasted_iota(jnp.int32, (theta_dev, LANES), 1)
+    for copy in far_planes:
+        copy.wait_send()
+    for plane, edge in ((0, 0), (planes + 1, slabs - 1)):
+        for f in range(FIELDS):
+            known = (lane_full >= NEAR) & (slab != edge)
+            state[0, f, plane, body, :] = jnp.where(known, state[0, f, plane, body, :], 0.0)
 
     def advance(tile, k):
         radius = (lane_row + tile * LANES).astype(jnp.float32) + 0.5
@@ -453,32 +457,37 @@
             across[f, k, 0:half, :] = first
             across[f, k, half:, :] = second
 
-    for copy in far_planes:
-        copy.wait_send()
-
-    def unpack_ghosts():
+    def add_ghosts():
         updates = []
-        for side, plane, edge in ((0, 0, 0), (1, planes + 1, slabs - 1)):
-            inside = slab != edge
-            tail0 = state[0, 4, plane, TOP:middle, :]
-            tail1 = state[0, 4, plane, middle : middle + half, :]
+        spread_rate = time_step * viscosity
+        for side, k, edge in ((0, 0, 0), (1, planes - 1, slabs - 1)):
+            sign = 0.5 * time_step * (1 - 2 * side)
+            inside = is_near & (slab != edge)
+            rate0 = spread_rate + sign * state[0, 2, k + 1, TOP:middle, :]
+            rate1 = spread_rate + sign * state[0, 2, k + 1, middle : middle + half, :]
+            tail0 = jnp.zeros((half, LANES), jnp.float32)
+            tail1 = tail0
+            parts = []
             for f in range(4):
                 got = ghost[side, f]
-                part0 = jnp.where(is_near, got, state[0, f, plane, TOP:middle, :])
-                part1 = jnp.where(
-                    is_near,
-                    pltpu.roll(got, HALF, 1),
-                    state[0, f, plane, middle : middle + half, :],
-                )
-                updates.append((f, plane, inside, part0, part1))
+                parts.append((f, got, pltpu.roll(got, HALF, 1)))
                 shift = (QUARTER * f - NEAR) % LANES
                 part = (lane >= QUARTER * f) & (lane < QUARTER * (f + 1))
                 tail0 = jnp.where(part, pltpu.roll(got, shift, 1), tail0)
                 tail1 = jnp.where(part, pltpu.roll(got, (shift + HALF) % LANES, 1), tail1)
-            updates.append((4, plane, inside, tail0, tail1))
-        for f, plane, inside, part0, part1 in updates:
-            state[0, f, plane, TOP:middle, :] = jnp.where(inside, part0, 0.0)
-            state[0, f, plane, middle : middle + half, :] = jnp.where(inside, part1, 0.0)
+            parts.append((4, tail0, tail1))
+            for f, part0, part1 in parts:
+                updates.append(
+                    (
+                        f,
+                        k,
+                        result[0, f, k, :half, :] + jnp.where(inside, part0 * rate0, 0.0),
+                        result[0, f, k, half:, :] + jnp.where(inside, part1 * rate1, 0.0),
+                    )
+                )
+        for f, k, part0, part1 in updates:
+            result[0, f, k, :half, :] = part0
+            result[0, f, k, half:, :] = part1
 
     whole(recv2, 8, 1, 8).wait_recv()
     for f in range(4):
@@ -494,24 +503,22 @@
     unpack([0, planes - 1])
     whole(recv2, sectors - 8, 1, 1).wait_recv()
 
-    def unpack_inner(i, carry):
-        unpack([1 + i * WIDE + step for step in range(WIDE)])
+    unpack([1, 2])
+
+    def near(i, carry):
+        advance(0, 2 * i - 2)
+        advance(0, 2 * i - 1)
+        unpack([2 * i + 1, 2 * i + 2])
         return carry
 
-    lax.fori_loop(0, (planes - 2) // WIDE, unpack_inner, 0)
-
-    def near(i, carry):
-        for step in range(WIDE2):
-            advance(0, 1 + i * WIDE2 + step)
-        return carry
-
-    lax.fori_loop(0, (planes - 2) // WIDE2, near, 0)
-    store(0, 1, planes - 2)
+    lax.fori_loop(1, planes // 2 - 1, near, 0)
+    store(0, 1, planes - 5)
+    for k in range(planes - 4, planes):
+        advance(0, k)
+    store(0, planes - 4, 3)
     for side in range(2):
         whole(ghost.at[side], 4, 6 + side, 6 + side).wait_recv()
-    unpack_ghosts()
-    advance(0, 0)
-    advance(0, planes - 1)
+    add_ghosts()
     store(0, 0, 1)
     store(0, planes - 1, 1)
     whole(send1, sectors, 0, 0).wait_send()
@@ -552,7 +559,7 @@
             pltpu.VMEM((2, tiles, count, planes, LANES), jnp.float32),
             pltpu.VMEM((2, tiles, count, planes, LANES), jnp.float32),
             pltpu.SemaphoreType.DMA((tiles + 2,)),
-            pltpu.SemaphoreType.DMA((tiles + 2,)),
+            pltpu.SemaphoreType.DMA((tiles + 3,)),
             pltpu.SemaphoreType.DMA((8,)),
             pltpu.SemaphoreType.DMA((9,)),
         ],

time: 34.9 us -> 34.8 us (level)
  no operation moved by 1% of the time
where the time goes in v7:
time: 34.8 us
  Pallas kernels  33.3 us (96%)
  local copies, waits for them, and re-layouts  1.49 us (4%)
    pallas_call x1, Pallas kernels, on_device(): pl.pallas_call(functools.partial(stencil_kernel, sectors, slabs), out_sha...  33.3 us
    unnamed x1, local copies, waits for them, and re-layouts  1.49 us

profile of v7, /device:TPU:1, one launch (start us, length us, event | category | flops | bytes accessed | tf_op | source)
XLA Modules:
  0.0 34.8 jit_solution(1585947850410446818)
XLA Ops:
  0.0 33.3 %plume_section.1 = f32[5,16,16,512]{3,2,1,0:T(8,128)S(1)} custom-call(f32[5,16,16,512]{3,2,1,0:T(8,128)} %fields.1, bf16[2,2,256,256]{3,2,1,0:T(8,128)(2,1)} %constant.4.clone.forward_hbm, bf16[2,3,288,256]{3,2,1,0:T(8,128)(2,1)} %constant.5.clone.inverse_hbm), custom_call_target="tpu_custom_call" | custom-call | tf_op jit(solution)/shard_map/plume_section/pallas_call | solution.py:542
  33.3 1.5 %copy.5 = f32[5,16,16,512]{3,2,1,0:T(8,128)} copy(f32[5,16,16,512]{3,2,1,0:T(8,128)S(1)} %plume_section.1) | data formatting | bytes 5242880

commit v8 on v6

--- a/solution.py
+++ b/solution.py
@@ -135,8 +135,8 @@
     around_z = [(own_z + step) % 8 for step in range(8)]
 
     def visit(call):
-        for step_x in (2, 1, 3, 0):
-            for step_z in (4, 0, 3, 1, 5, 7, 2, 6):
+        for step_x in (2, 3, 1, 0):
+            for step_z in (4, 7, 3, 1, 5, 0, 2, 6):
                 for step_y in range(2):
                     call(around_x[step_x] + around_y[step_y] + around_z[step_z])
 

time: 34.9 us -> 35 us (level)
  no operation moved by 1% of the time
where the time goes in v8:
time: 35 us; the launch traced here: 34.9 us
  Pallas kernels  33.4 us (95%)
  local copies, waits for them, and re-layouts  1.49 us (4%)
    pallas_call x1, Pallas kernels, on_device(): pl.pallas_call(functools.partial(stencil_kernel, sectors, slabs), out_sha...  33.4 us
    unnamed x1, local copies, waits for them, and re-layouts  1.49 us

profile of v8, /device:TPU:1, one launch (start us, length us, event | category | flops | bytes accessed | tf_op | source)
XLA Modules:
  0.0 34.9 jit_solution(16580516348122111939)
XLA Ops:
  0.0 33.4 %plume_section.1 = f32[5,16,16,512]{3,2,1,0:T(8,128)S(1)} custom-call(f32[5,16,16,512]{3,2,1,0:T(8,128)} %fields.1, bf16[2,2,256,256]{3,2,1,0:T(8,128)(2,1)} %constant.4.clone.forward_hbm, bf16[2,3,288,256]{3,2,1,0:T(8,128)(2,1)} %constant.5.clone.inverse_hbm), custom_call_target="tpu_custom_call" | custom-call | tf_op jit(solution)/shard_map/plume_section/pallas_call | solution.py:535
  33.4 1.5 %copy.5 = f32[5,16,16,512]{3,2,1,0:T(8,128)} copy(f32[5,16,16,512]{3,2,1,0:T(8,128)S(1)} %plume_section.1) | data formatting | bytes 5242880

commit v9 on v6

--- a/solution.py
+++ b/solution.py
@@ -396,10 +396,11 @@
     for tile in range(1, tiles):
 
         def far(k, carry):
-            advance(tile, k)
+            advance(tile, 2 * k + 0)
+            advance(tile, 2 * k + 1)
             return carry
 
-        lax.fori_loop(0, planes, far, 0)
+        lax.fori_loop(0, planes // 2, far, 0)
         store(tile, 0, planes)
 
     sublane = lax.broadcasted_iota(jnp.int32, (half, LANES), 0)

time: 34.9 us -> 34.9 us (level)
  no operation moved by 1% of the time
where the time goes in v9:
time: 34.9 us; the launch traced here: 34.8 us
  Pallas kernels  33.3 us (95%)
  local copies, waits for them, and re-layouts  1.49 us (4%)
    pallas_call x1, Pallas kernels, on_device(): pl.pallas_call(functools.partial(stencil_kernel, sectors, slabs), out_sha...  33.3 us
    unnamed x1, local copies, waits for them, and re-layouts  1.49 us

profile of v9, /device:TPU:1, one launch (start us, length us, event | category | flops | bytes accessed | tf_op | source)
XLA Modules:
  0.0 34.8 jit_solution(506901408358400892)
XLA Ops:
  0.0 33.3 %plume_section.1 = f32[5,16,16,512]{3,2,1,0:T(8,128)S(1)} custom-call(f32[5,16,16,512]{3,2,1,0:T(8,128)} %fields.1, bf16[2,2,256,256]{3,2,1,0:T(8,128)(2,1)} %constant.4.clone.forward_hbm, bf16[2,3,288,256]{3,2,1,0:T(8,128)(2,1)} %constant.5.clone.inverse_hbm), custom_call_target="tpu_custom_call" | custom-call | tf_op jit(solution)/shard_map/plume_section/pallas_call | solution.py:536
  33.3 1.5 %copy.5 = f32[5,16,16,512]{3,2,1,0:T(8,128)} copy(f32[5,16,16,512]{3,2,1,0:T(8,128)S(1)} %plume_section.1) | data formatting | bytes 5242880
